TPU v7x, 32 devices: a whole 2x2x4 slice. The times are simulated.
32 devices in a mesh: grid: 8 (over z, y), tile: 4 (over x, core).
Axes of the slice: x: 2, y: 2, z: 4, core: 2. Of those that a mesh axis runs over, the one named last changes fastest.
Arguments:
- point_values: bfloat16 [256, 16384], P('grid', 'tile'), may hold values from -1.75 to 1.75
- sig_blocks: int32 [8, 16], P('grid'), may hold values from 0 to 31, as said below
- density: bfloat16 [16384, 16384], P('grid', 'tile'), may hold values from -0.0625 to 0.0625
- coulomb_core: bfloat16 [512, 512], replicated, may hold values from -0.25 to 0.25
- screen_mask: int32 [32, 32], replicated, may hold values 0 or 1
- ao_centers: float32 [3, 16384], replicated, may hold values from -1 to 1
- ao_widths: float32 [16384], replicated, may hold values from 0.25 to 1
- point_coords: float32 [3, 256], P(None, 'grid'), may hold values from -1 to 1
- lmo_coeffs: bfloat16 [16384, 1024], P('tile'), may hold values from -0.0625 to 0.0625
- domain_blocks: int32 [4, 16], replicated, may hold values from 0 to 31, as said below
Outputs:
- half: bfloat16 [1024, 16384], P('tile', 'grid')
Inputs may be any that keep to these rules, and one draw needn't show every extreme that they name: `sig_blocks`: each batch names 16 different AO blocks. `domain_blocks`: each strip's 16 blocks are different, and every AO block lies in the domain of some strip.
All inputs are finite; a program needn't handle non-finite values.
Results may differ from a plain program's by a relative error of at most 0.02.
Values may be sent and summed in bfloat16 or wider, within the bound.
A program may use at most 128 MiB of HBM per device.

v0:
```python
import functools
import math

import jax
import jax.numpy as jnp
from jax import lax
from jax.experimental import pallas as pl
from jax.experimental.pallas import tpu as pltpu
from jax.sharding import PartitionSpec as P

MESH = pl.DeviceIdType.MESH
VMEM_LIMIT = 60 * 1024 * 1024
f32 = jnp.float32
bf16 = jnp.bfloat16


def grid_split(grid_count):
    inner = max(1, math.isqrt(max(1, grid_count // 2)))
    while grid_count % inner:
        inner -= 1
    return grid_count // inner, inner


def tile_split(tile_count):
    inner = 2 if tile_count % 2 == 0 else 1
    return tile_count // inner, inner


def remote(src, dst, send_sem, recv_sem, device):
    return pltpu.make_async_remote_copy(
        src_ref=src,
        dst_ref=dst,
        send_sem=send_sem,
        recv_sem=recv_sem,
        device_id=device,
        device_id_type=MESH,
    )


def greet(devices, work=None):
    barrier = pltpu.get_barrier_semaphore()
    for device in devices:
        pl.semaphore_signal(barrier, inc=1, device_id=device, device_id_type=MESH)
    if work is not None:
        work()
    pl.semaphore_wait(barrier, len(devices))


def params(collective_id):
    return pltpu.CompilerParams(
        collective_id=collective_id, has_side_effects=True, vmem_limit_bytes=VMEM_LIMIT
    )


def vmem():
    return pl.BlockSpec(memory_space=pltpu.VMEM)


def listed(table_ref, row, block_id):
    flag = jnp.float32(0.0)
    for i in range(table_ref.shape[1]):
        flag = jnp.where(table_ref[row, i] == block_id, jnp.float32(1.0), flag)
    return flag


def front_kernel(
    block_size,
    grid_count,
    tile_count,
    sig_ref,
    value_ref,
    density_hbm,
    out_ref,
    rows_ref,
    x_ref,
    all_ref,
    density_ref,
    part_ref,
    sibling_ref,
    pair_ref,
    peer_ref,
    total_ref,
    zs,
    zr,
    ys,
    yr,
    es,
    er,
    local_sem,
    ds,
    cs,
    cr,
    xs,
    xr,
    gs,
    gr,
):
    chunks, slab, width = part_ref.shape[0], part_ref.shape[4], part_ref.shape[5]
    loads = [
        pltpu.make_async_copy(
            density_hbm.at[pl.ds(i * width, width)],
            density_ref.at[pl.ds(i * width, width)],
            ds.at[i],
        )
        for i in range(chunks)
    ]
    g, t = lax.axis_index("grid"), lax.axis_index("tile")
    nz, ny = grid_split(grid_count)
    nx, nc = tile_split(tile_count)
    z, y = g // ny, g % ny
    x, c = t // nc, t % nc
    cols = x_ref.shape[1]
    rows = rows_ref.shape[2]
    offset = pl.multiple_of((g * rows) % cols, rows)
    owner = (g * rows) // cols
    is_owner = owner == t
    in_column = owner % nc == c
    has_left, has_right = z > 0, z < nz - 1
    left = (lax.rem(z + nz - 1, nz) * ny + y, t)
    right = (lax.rem(z + 1, nz) * ny + y, t)
    y_peers = [(z * ny + lax.rem(y + d, ny), t) for d in range(1, ny)]
    x_peers = [(g, lax.rem(x + d, nx) * nc + c) for d in range(1, nx)]
    c_peers = [(g, x * nc + (1 - c))] if nc == 2 else []
    g_peers = [(lax.rem(g + d, grid_count), t) for d in range(1, grid_count)]

    def make_mask():
        for m in range(cols // block_size):
            lanes = slice(m * block_size, (m + 1) * block_size)
            flag = listed(sig_ref, 0, t * (cols // block_size) + m)
            x_ref[:, lanes] = (value_ref[:, lanes].astype(f32) * flag).astype(bf16)

    greet(g_peers + x_peers + c_peers, make_mask)

    def present(k):
        if k == 0:
            return z >= 0
        step = (k + 1) // 2
        return z >= step if k % 2 else z <= nz - 1 - step

    def source(k, d):
        step = (k + 1) // 2
        line = lax.rem(z + nz - step, nz) if k % 2 else lax.rem(z + step, nz)
        return line * ny + lax.rem(y + ny - d, ny)

    def block(k, d):
        return x_ref if k == 0 and d == 0 else all_ref.at[source(k, d)]

    def along(k, to_right):
        step = (k + 1) // 2
        lane = 0 if to_right else 1
        return remote(
            block(k, 0),
            all_ref.at[source(k, 0)],
            zs.at[lane, step],
            zr.at[lane, step],
            right if to_right else left,
        )

    def across(k, d):
        return remote(
            block(k, 0), all_ref.at[source(k, 0)], ys.at[d, k], yr.at[d, k], y_peers[d - 1]
        )

    def arrived(k, d, sends, recvs):
        spot = all_ref.at[source(k, d)]
        remote(spot, spot, sends, recvs, right).wait_recv()

    def share(k, d):
        for i, peer in enumerate(x_peers + c_peers):
            remote(
                block(k, d).at[:, pl.ds(offset, rows)],
                rows_ref.at[source(k, d)],
                es.at[i],
                er.at[d, k],
                peer,
            ).start()

    steps = range(2 * nz - 1)

    def send_block(k):
        if k == 0 or k % 2:

            @pl.when(has_right)
            def _():
                along(k, True).start()

        if k == 0 or k % 2 == 0:

            @pl.when(has_left)
            def _():
                along(k, False).start()

        for d in range(1, ny):
            across(k, d).start()

        @pl.when(is_owner)
        def _():
            share(k, 0)

    def take_across(k):
        @pl.when(present(k))
        def _():
            for d in range(1, ny):
                arrived(k, d, ys.at[d, k], yr.at[d, k])

                @pl.when(is_owner)
                def _():
                    share(k, d)

    batch = x_ref.shape[0]

    def product(i):
        loads[i].wait()
        value = lax.dot_general(
            all_ref[...].reshape(grid_count * batch, cols),
            density_ref[i * width : (i + 1) * width, :],
            (((1,), (1,)), ((), ())),
            preferred_element_type=f32,
        )
        if slab % 8 == 0:
            part_ref[i] = value.reshape(grid_count, nx, nc, slab, width).astype(bf16)
        else:
            for n in range(grid_count * batch // slab):
                part_ref[i, n // (nx * nc), n // nc % nx, n % nc] = value[
                    n * slab : (n + 1) * slab
                ].astype(bf16)

    send_block(0)
    keep = pltpu.make_async_copy(x_ref, all_ref.at[g], local_sem)
    keep.start()
    for load in loads:
        load.start()
    for step in range(1, nz):
        for k in (2 * step - 1, 2 * step):

            @pl.when(present(k))
            def _():
                lane = 0 if k % 2 else 1
                arrived(k, 0, zs.at[lane, step - 1], zr.at[lane, step - 1])
                send_block(k)

        if step == 1:
            take_across(0)
        else:
            take_across(2 * step - 3)
            take_across(2 * step - 2)
    if nz > 1:
        take_across(2 * nz - 3)
        take_across(2 * nz - 2)
    else:
        take_across(0)
    keep.wait()
    order = list(range(1, nx)) + [0]

    def core_copy(i, d):
        column = lax.rem(x + d, nx)
        return remote(
            part_ref.at[i, :, column, 1 - c],
            sibling_ref.at[i, :, column],
            cs.at[i, d],
            cr.at[i, d],
            c_peers[0],
        )

    def pair_copy(i, d):
        return remote(
            pair_ref.at[i, d], peer_ref.at[i, d], xs.at[i, d], xr.at[i, d], x_peers[d - 1]
        )

    def exchange(i):
        for d in order:
            column = lax.rem(x + d, nx)
            if nc == 2:
                core_copy(i, d).wait_recv()

            @pl.loop(0, grid_count)
            def _(n):
                value = part_ref[i, n, column, c].astype(f32)
                if nc == 2:
                    value = value + sibling_ref[i, n, column].astype(f32)
                pair_ref[i, d, n] = value.astype(bf16)

            if d:
                pair_copy(i, d).start()

    def pass_rows():
        @pl.when(jnp.logical_not(is_owner))
        def _():
            for k in steps:

                @pl.when(present(k))
                def _():
                    for d in range(ny):
                        spot = rows_ref.at[source(k, d)]
                        pass_on = remote(
                            spot, spot, es.at[nx - 1], er.at[d, k], (c_peers or [right])[0]
                        )
                        if nc == 2:

                            @pl.when(in_column)
                            def _():
                                pass_on.wait_recv()
                                pass_on.start()

    own = pltpu.make_async_copy(all_ref.at[:, :, pl.ds(offset, rows)], rows_ref, local_sem)

    @pl.when(is_owner)
    def _():
        own.start()

    for i in range(chunks):
        product(i)
        if nc == 2:
            for d in order:
                core_copy(i, d).start()
        if i == 0:
            pass_rows()
        else:
            exchange(i - 1)
    exchange(chunks - 1)

    for i in range(chunks):
        for d in range(1, nx):
            pair_copy(i, d).wait_recv()

        @pl.loop(0, grid_count)
        def _(n):
            value = pair_ref[i, 0, n].astype(f32)
            for d in range(1, nx):
                value = value + peer_ref[i, d, n].astype(f32)
            total_ref[n, :, i * width : (i + 1) * width] = value.astype(bf16)

    g_copies = []
    for d in range(1, grid_count):
        target = lax.rem(g + d, grid_count)
        copy = remote(
            total_ref.at[target], out_ref.at[g], gs.at[d], gr.at[d], g_peers[d - 1]
        )
        copy.start()
        g_copies.append(copy)
    out_ref[g] = total_ref[g]

    @pl.when(is_owner)
    def _():
        for i in range(len(x_peers + c_peers)):
            remote(rows_ref, rows_ref, es.at[i], er.at[0, 0], right).wait_send()
        own.wait()

    if nc == 2:

        @pl.when(jnp.logical_and(in_column, jnp.logical_not(is_owner)))
        def _():
            remote(rows_ref, rows_ref, es.at[nx - 1], er.at[0, 0], right).wait_send()

        waits_rows = jnp.logical_not(in_column)
    else:
        waits_rows = jnp.logical_not(is_owner)

    @pl.when(waits_rows)
    def _():
        for k in steps:

            @pl.when(present(k))
            def _():
                for d in range(ny):
                    spot = rows_ref.at[source(k, d)]
                    remote(spot, spot, es.at[0], er.at[d, k], right).wait_recv()

    for k in steps:

        @pl.when(present(k))
        def _():
            if k == 0 or k % 2:

                @pl.when(has_right)
                def _():
                    along(k, True).wait_send()

            if k == 0 or k % 2 == 0:

                @pl.when(has_left)
                def _():
                    along(k, False).wait_send()

            for d in range(1, ny):
                across(k, d).wait_send()

    for i in range(chunks):
        for d in range(nx):
            if nc == 2:
                core_copy(i, d).wait_send()
            if d:
                pair_copy(i, d).wait_send()
    for copy in g_copies:
        copy.wait()


def smem():
    return pl.BlockSpec(memory_space=pltpu.SMEM)


def front(sig_blocks, values, density, block_size, grid_count, tile_count):
    batch, cols = values.shape
    rows = density.shape[0]
    nz, ny = grid_split(grid_count)
    nx, nc = tile_split(tile_count)
    slab = batch // tile_count
    width = min(rows, 512)
    chunks = rows // width
    dma = pltpu.SemaphoreType.DMA
    return pl.pallas_call(
        functools.partial(front_kernel, block_size, grid_count, tile_count),
        out_shape=(
            jax.ShapeDtypeStruct((grid_count, slab, rows), bf16),
            jax.ShapeDtypeStruct((grid_count, batch, rows), bf16),
        ),
        in_specs=[smem(), vmem(), pl.BlockSpec(memory_space=pl.ANY)],
        out_specs=(vmem(), vmem()),
        scratch_shapes=[
            pltpu.VMEM((batch, cols), bf16),
            pltpu.VMEM((grid_count, batch, cols), bf16),
            pltpu.VMEM((rows, cols), bf16),
            pltpu.VMEM((chunks, grid_count, nx, nc, slab, width), bf16),
            pltpu.VMEM((chunks, grid_count, nx, slab, width), bf16),
            pltpu.VMEM((chunks, nx, grid_count, slab, width), bf16),
            pltpu.VMEM((chunks, nx, grid_count, slab, width), bf16),
            pltpu.VMEM((grid_count, slab, rows), bf16),
            dma((2, nz)),
            dma((2, nz)),
            dma((ny, 2 * nz)),
            dma((ny, 2 * nz)),
            dma((nx,)),
            dma((ny, 2 * nz)),
            dma,
            dma((chunks,)),
            dma((chunks, nx)),
            dma((chunks, nx)),
            dma((chunks, nx)),
            dma((chunks, nx)),
            dma((grid_count,)),
            dma((grid_count,)),
        ],
        compiler_params=params(0),
    )(sig_blocks, values, density)


def finish_kernel(
    grid_count,
    tile_count,
    pot_ref,
    lmo_hbm,
    domain_ref,
    all_ref,
    lmo_ref,
    got_ref,
    flat_ref,
    send_ref,
    part_ref,
    own_ref,
    lmo_sem,
    vs,
    vr,
    ws,
    wr,
    gs,
    gr,
):
    g, t = lax.axis_index("grid"), lax.axis_index("tile")
    load = pltpu.make_async_copy(lmo_hbm, lmo_ref, lmo_sem)
    load.start()
    t_peers = [(g, lax.rem(t + d, tile_count)) for d in range(1, tile_count)]
    g_peers = [(lax.rem(g + d, grid_count), t) for d in range(1, grid_count)]
    greet(t_peers + g_peers)
    cols = got_ref.shape[1]
    strips = domain_ref.shape[0]
    slab = pot_ref.shape[1]
    block = pot_ref.shape[2]
    strip = own_ref.shape[1]

    v_copies = []
    for d in range(1, tile_count):
        target = lax.rem(t + d, tile_count)
        copy = remote(
            pot_ref.at[pl.ds(target * cols, cols)],
            got_ref.at[t],
            vs.at[d],
            vr.at[d],
            t_peers[d - 1],
        )
        copy.start()
        v_copies.append(copy)
    got_ref[t] = pot_ref[pl.ds(t * cols, cols)]
    flags = [[listed(domain_ref, s, t * cols + m) for m in range(cols)] for s in range(strips)]
    for copy in v_copies:
        copy.wait()
    for i in range(tile_count):
        for m in range(cols):
            flat_ref[m, i * slab : (i + 1) * slab, :] = got_ref[i, m].astype(f32)
    load.wait()
    width = lmo_ref.shape[1] // strips
    per_tile = strips // tile_count
    for s in range(strips):
        lanes = slice(s * width, (s + 1) * width)
        total = None
        for m in range(cols):
            term = flags[s][m] * jnp.dot(
                flat_ref[m].astype(bf16),
                lmo_ref[m * block : (m + 1) * block, lanes],
                preferred_element_type=f32,
            )
            total = term if total is None else total + term
        first = s % per_tile * width
        send_ref[s // per_tile, :, first : first + width] = total.astype(bf16)
    w_copies = []
    for d in range(1, tile_count):
        target = lax.rem(t + d, tile_count)
        copy = remote(
            send_ref.at[target], part_ref.at[d], ws.at[d], wr.at[d], t_peers[d - 1]
        )
        copy.start()
        w_copies.append(copy)
    total = send_ref[t].astype(f32)
    for d, copy in enumerate(w_copies):
        copy.wait()
        total = total + part_ref[d + 1].astype(f32)
    own_ref[...] = total.astype(bf16)
    g_copies = []
    for d in range(1, grid_count):
        copy = remote(own_ref, all_ref.at[g], gs.at[d], gr.at[d], g_peers[d - 1])
        copy.start()
        g_copies.append(copy)
    all_ref[g] = own_ref[...]
    for copy in g_copies:
        copy.wait()


def finish(potential, lmo_coeffs, domain_blocks, batch, grid_count, tile_count):
    blocks, slab, block = potential.shape
    cols = blocks // tile_count
    total = lmo_coeffs.shape[1]
    strip = total // tile_count
    dma = pltpu.SemaphoreType.DMA
    return pl.pallas_call(
        functools.partial(finish_kernel, grid_count, tile_count),
        out_shape=jax.ShapeDtypeStruct((grid_count, batch, strip), bf16),
        in_specs=[vmem(), pl.BlockSpec(memory_space=pl.ANY), smem()],
        out_specs=vmem(),
        scratch_shapes=[
            pltpu.VMEM(lmo_coeffs.shape, bf16),
            pltpu.VMEM((tile_count, cols, slab, block), bf16),
            pltpu.VMEM((cols, batch, block), f32),
            pltpu.VMEM((tile_count, batch, strip), bf16),
            pltpu.VMEM((tile_count, batch, strip), bf16),
            pltpu.VMEM((batch, strip), bf16),
            dma,
            dma((tile_count,)),
            dma((tile_count,)),
            dma((tile_count,)),
            dma((tile_count,)),
            dma((grid_count,)),
            dma((grid_count,)),
        ],
        compiler_params=params(2),
    )(potential, lmo_coeffs, domain_blocks)


def shards(
    point_values,
    sig_blocks,
    density,
    coulomb_core,
    screen_mask,
    ao_centers,
    ao_widths,
    point_coords,
    lmo_coeffs,
    domain_blocks,
):
    grid_count = lax.axis_size("grid")
    tile_count = lax.axis_size("tile")
    panel = lax.axis_index("tile")
    own_rows, own_cols = density.shape
    points = point_values.shape[0]
    block_size = coulomb_core.shape[0]
    total_aos = ao_widths.shape[0]
    all_blocks = total_aos // block_size
    slab = points // tile_count
    block_ids = jnp.arange(all_blocks, dtype=jnp.int32)
    named = jnp.any(sig_blocks[0][:, None] == block_ids[None, :], axis=0)
    summed, row_values = front(
        sig_blocks, point_values, density, block_size, grid_count, tile_count
    )
    row_blocks = own_rows // block_size
    term = summed.astype(f32).reshape(grid_count, slab, row_blocks, block_size)
    term = jnp.transpose(term, (0, 2, 1, 3)).reshape(all_blocks, slab, block_size)
    coords = lax.dynamic_slice_in_dim(point_coords, panel * slab, slab, 1)
    offsets = (
        ao_centers.reshape(3, all_blocks, 1, block_size) - coords.reshape(3, 1, slab, 1)
    )
    coefficient = 1.0 / jnp.sqrt(
        jnp.sum(offsets * offsets, axis=0) + ao_widths.reshape(all_blocks, 1, block_size)
    )
    scaled = coefficient * named.astype(f32)[:, None, None]
    weighted = (scaled * term).astype(bf16)
    screened = jnp.einsum(
        "kj,jpa->kpa", screen_mask.astype(bf16), weighted, preferred_element_type=f32
    ).astype(bf16)
    mixed = jnp.einsum(
        "kpc,ac->kpa", screened, coulomb_core, preferred_element_type=f32
    )
    potential = (scaled * mixed).astype(bf16)
    weights = finish(potential, lmo_coeffs, domain_blocks, points, grid_count, tile_count)
    return lax.dot_general(
        weights.reshape(grid_count * points, weights.shape[2]),
        row_values.reshape(grid_count * points, own_rows),
        (((0,), (0,)), ((), ())),
        preferred_element_type=f32,
    ).astype(bf16)


def solution(mesh):
    in_specs = (
        P("grid", "tile"),
        P("grid", None),
        P("grid", "tile"),
        P(),
        P(),
        P(),
        P(),
        P(None, "grid"),
        P("tile", None),
        P(),
    )
    out_specs = P("tile", "grid")
    return jax.shard_map(shards, mesh=mesh, in_specs=in_specs, out_specs=out_specs, check_vma=False)
```

profile of v0, /device:TPU:0, one launch (start us, length us, event | category | flops | bytes accessed | tf_op | source)
XLA Modules:
  0.0 75.7 jit_solution(2229496818821122926)
XLA Ops:
  0.0 0.0 copy-start
  0.0 51.2 %shard_map.100 = (bf16[8,8,2048]{2,1,0:T(8,128)(2,1)}, bf16[8,32,2048]{2,1,0:T(8,128)(2,1)}) custom-call(s32[1,16]{1,0:T(1,128)} %sig_ref.1, bf16[32,4096]{1,0:T(8,128)(2,1)} %value_ref.1, bf16[2048,4096]{1,0:T(8,128)(2,1)} %density_hbm.1), custom_call_target="tpu_custom_call" | custom-call | tf_op jit(solution)/shard_map/pallas_call | solution.py:411
  51.2 0.0 copy-start.4
  51.2 0.0 copy-start.1
  51.2 0.0 copy-start.2
  51.2 0.0 copy-start.5
  51.2 1.0 %fusion.9 = (f32[8,8,512]{2,1,0:T(8,128)S(1)}, f32[8,8,512]{2,1,0:T(8,128)S(1)}, f32[8,8,512]{2,1,0:T(8,128)S(1)}, f32[8,8,512]{2,1,0:T(8,128)S(1)}) fusion(bf16[8,8,2048]{2,1,0:T(8,128)(2,1)} %get-tuple-element.7), kind=kLoop, calls=%fused_computation.19 | loop fusion | bytes 1048576 | tf_op jit(solution)/shard_map/slice
  52.3 0.0 copy-start.3
  52.3 0.0 copy-done.4
  52.3 0.1 constant_dynamic-slice_fusion
  52.4 0.0 copy-done.1
  52.4 0.1 copy.19
  52.5 0.2 multiply_reduce_fusion
  52.7 0.0 copy-done.2
  52.8 0.0 copy-done.5
  52.8 0.1 fusion.8
  52.9 0.1 multiply_convert_fusion
  53.0 0.1 copy-done.3
  53.0 0.2 fusion.2
  53.3 0.0 copy-done
  53.3 1.0 %fusion.1.pot_ref = bf16[32,8,512]{2,1,0:T(8,128)(2,1)} fusion(bf16[512,512]{1,0:T(8,128)(2,1)S(1)} %copy-done, f32[32,8,512]{2,1,0:T(8,128)S(1)} %multiply_reduce_fusion, bf16[32,8,512]{2,0,1:T(8,128)(2,1)S(1)} %fusion.2, f32[32]{0:T(128)S(1)} %convert_element_type.28, f32[32,512]{1,0:T(8,128)S(1)} %add.14), kind=kOutput, calls=%fused_computation.4 | convolution fusion | flops 134742016 | bytes 1638528 | tf_op jit(solution)/shard_map/kpc,ac->kpa/dot_general | solution.py:608
  54.3 0.0 copy-start.6
  54.3 19.0 %shard_map.101 = bf16[8,32,256]{2,1,0:T(8,128)(2,1)} custom-call(bf16[32,8,512]{2,1,0:T(8,128)(2,1)} %fusion.1.pot_ref, bf16[4096,1024]{1,0:T(8,128)(2,1)} %lmo_hbm.1, s32[4,16]{1,0:T(4,128)} %domain_ref.1), custom_call_target="tpu_custom_call" | custom-call | tf_op jit(solution)/shard_map/pallas_call | solution.py:543
  73.3 0.0 copy-done.6
  73.3 2.3 %fusion = bf16[256,2048]{1,0:T(8,128)(2,1)} fusion(bf16[8,32,256]{2,1,0:T(8,128)(2,1)} %shard_map.101, bf16[8,32,2048]{2,1,0:T(8,128)(2,1)S(1)} %copy-done.6), kind=kOutput, calls=%fused_computation.1 | convolution fusion | flops 268959744 | bytes 2228224 | tf_op jit(solution)/shard_map/dot_general | solution.py:613
  (3 shorter events, 0.1 us)
Async XLA Ops:
  0.0 53.3 %copy-start = (bf16[512,512]{1,0:T(8,128)(2,1)S(1)}, bf16[512,512]{1,0:T(8,128)(2,1)}, u32[]{:S(2)}) copy-start(bf16[512,512]{1,0:T(8,128)(2,1)} %param.13) | copy-start | bytes 1572868
  51.2 1.2 %copy-start.4 = (f32[3,32]{1,0:T(4,128)S(1)}, f32[3,32]{1,0:T(4,128)}, u32[]{:S(2)}) copy-start(f32[3,32]{1,0:T(4,128)} %param.17) | copy-start | bytes 1156
  51.2 1.2 %copy-start.1 = (f32[3,16384]{1,0:T(4,128)S(1)}, f32[3,16384]{1,0:T(4,128)}, u32[]{:S(2)}) copy-start(f32[3,16384]{1,0:T(4,128)} %param.15) | copy-start | bytes 589828
  51.2 1.5 %copy-start.2 = (f32[16384]{0:T(1024)S(1)}, f32[16384]{0:T(1024)}, u32[]{:S(2)}) copy-start(f32[16384]{0:T(1024)} %param.16) | copy-start | bytes 196612
  51.2 1.5 %copy-start.5 = (s32[1,16]{1,0:T(1,128)S(1)}, s32[1,16]{1,0:T(1,128)}, u32[]{:S(2)}) copy-start(s32[1,16]{1,0:T(1,128)} %sig_ref.1) | copy-start | bytes 196
  52.3 0.7 copy-start.3
  54.3 19.0 %copy-start.6 = (bf16[8,32,2048]{2,1,0:T(8,128)(2,1)S(1)}, bf16[8,32,2048]{2,1,0:T(8,128)(2,1)}, u32[]{:S(2)}) copy-start(bf16[8,32,2048]{2,1,0:T(8,128)(2,1)} %get-tuple-element.8) | copy-start | bytes 3145732
where the time goes:
time: 75.9 us; the launch traced here: 75.7 us
  Pallas kernels  70.1 us (92%)
  matrix products  3.61 us (5%)
  local copies, waits for them, and re-layouts  1.27 us (2%)
    pallas_call x1, Pallas kernels, front(): pl.pallas_call(functools.partial(front_kernel, block_size, grid_count, ti...  51.2 us
    pallas_call x1, Pallas kernels, finish(): pl.pallas_call(functools.partial(finish_kernel, grid_count, tile_count),...  19 us
    dot_general x1, matrix products, shards(): lax.dot_general(weights.reshape(grid_count * points, weights.shape[2]), r...  2.34 us

commit v1 on v0

v1 whole, which is shorter than its diff:
```python
import functools
import math

import jax
import jax.numpy as jnp
from jax import lax
from jax.experimental import pallas as pl
from jax.experimental.pallas import tpu as pltpu
from jax.sharding import PartitionSpec as P

MESH = pl.DeviceIdType.MESH
VMEM_LIMIT = 60 * 1024 * 1024
CHUNK = 512
EARLY = 1
LAG = 3
f32 = jnp.float32
bf16 = jnp.bfloat16
NT = (((1,), (1,)), ((), ()))
TN = (((0,), (0,)), ((), ()))


def grid_split(grid_count):
    inner = max(1, math.isqrt(max(1, grid_count // 2)))
    while grid_count % inner:
        inner -= 1
    return grid_count // inner, inner


def remote(src, dst, send_sem, recv_sem, device):
    return pltpu.make_async_remote_copy(
        src_ref=src,
        dst_ref=dst,
        send_sem=send_sem,
        recv_sem=recv_sem,
        device_id=device,
        device_id_type=MESH,
    )


def listed(table_ref, row, block_id):
    flag = jnp.float32(0.0)
    for i in range(table_ref.shape[1]):
        flag = jnp.where(table_ref[row, i] == block_id, jnp.float32(1.0), flag)
    return flag


def dot(a, b, dims=(((1,), (0,)), ((), ()))):
    return lax.dot_general(a, b, dims, preferred_element_type=f32)


def kernel(
    nz,
    ny,
    nx,
    sig_ref,
    domain_ref,
    value_ref,
    density_hbm,
    core_hbm,
    mask_hbm,
    centers_hbm,
    widths_hbm,
    coords_hbm,
    lmo_hbm,
    out_ref,
    all_ref,
    density_ref,
    acc_ref,
    part_ref,
    sibling_ref,
    pair_ref,
    peer_ref,
    total_ref,
    back_ref,
    core_ref,
    mask_ref,
    centers_ref,
    widths_ref,
    coords_ref,
    lmo_ref,
    scaled_ref,
    spread_ref,
    weighted_ref,
    pot_ref,
    got_ref,
    flat_ref,
    send_ref,
    share_ref,
    own_ref,
    weights_ref,
    rows_ref,
    flags_ref,
    zs,
    zr,
    ds_,
    dr,
    ys,
    yr,
    es,
    er,
    local_sem,
    load_sem,
    cs,
    cr,
    xs,
    xr,
    gs,
    gr,
    vs,
    vr,
    ws,
    wr,
    fs,
    fr,
):
    grid_count, tile_count, nc = nz * ny, nx * 2, 2
    batch, cols = value_ref.shape
    rows = density_ref.shape[0]
    block = core_ref.shape[0]
    blocks = mask_ref.shape[0]
    slab = batch // tile_count
    tile_blocks = cols // block
    row_blocks = rows // block
    chunks = cols // CHUNK
    strips = domain_ref.shape[0]
    strip_width = lmo_ref.shape[1] // strips
    per_tile = strips // tile_count

    g, t = lax.axis_index("grid"), lax.axis_index("tile")
    z, y = g // ny, g % ny
    x, c = t // nc, t % nc
    place = c * nx + x
    has_left, has_right = z > 0, z < nz - 1
    left = (lax.rem(z + nz - 1, nz) * ny + y, t)
    right = (lax.rem(z + 1, nz) * ny + y, t)
    y_peers = [(z * ny + lax.rem(y + d, ny), t) for d in range(1, ny)]
    x_peers = [(g, lax.rem(x + d, nx) * nc + c) for d in range(1, nx)]
    sibling = (g, x * nc + (1 - c))
    far_tiles = [
        lax.rem(x + d, nx) * nc + (c if e == 0 else 1 - c) for d in range(1, nx) for e in range(nc)
    ]
    tile_order = far_tiles + [x * nc + (1 - c), t]

    loads = [
        pltpu.make_async_copy(src, dst, load_sem.at[i])
        for i, (src, dst) in enumerate(
            [
                (coords_hbm, coords_ref),
                (widths_hbm, widths_ref),
                (centers_hbm, centers_ref),
                (mask_hbm, mask_ref),
                (core_hbm, core_ref),
                (density_hbm, density_ref),
                (lmo_hbm, lmo_ref),
            ]
        )
    ]
    small_loads, core_load, density_load, lmo_load = loads[:4], loads[4], loads[5], loads[6]

    barrier = pltpu.get_barrier_semaphore()

    def hello(device):
        pl.semaphore_signal(barrier, inc=1, device_id=device, device_id_type=MESH)

    @pl.when(has_left)
    def _():
        hello(left)

    @pl.when(has_right)
    def _():
        hello(right)

    for peer in y_peers + [(g, tile) for tile in tile_order[:-1]]:
        hello(peer)

    for m in range(tile_blocks):
        lanes = slice(m * block, (m + 1) * block)
        flag = listed(sig_ref, 0, t * tile_blocks + m)
        all_ref[g, :, lanes] = (value_ref[:, lanes].astype(f32) * flag).astype(bf16)

    neighbours = (
        ny - 1 + tile_count - 1 + jnp.where(has_left, 1, 0) + jnp.where(has_right, 1, 0)
    )
    pl.semaphore_wait(barrier, neighbours)

    def source(line, d):
        return line * ny + lax.rem(y + ny - d, ny)

    def piece(src, q):
        return all_ref.at[src, :, pl.ds(q * CHUNK, CHUNK)]

    def z_sems(lane, line, d, q):
        if d == 0:
            return zs.at[lane, line], zr.at[lane, line, q]
        return ds_.at[lane, line, d - 1], dr.at[lane, line, d - 1, q]

    def along(line, d, q, lane):
        spot = piece(source(line, d), q)
        send, recv = z_sems(lane, line, d, q)
        return remote(spot, spot, send, recv, left if lane else right)

    def across(line, d, q):
        spot = piece(source(line, 0), q)
        return remote(spot, spot, ys.at[d - 1, line], yr.at[d - 1, line, q], y_peers[d - 1])

    def along_arrived(line, d, q, lane):
        spot = piece(source(line, d), q)
        send, recv = z_sems(lane, line, d, q)
        remote(spot, spot, send, recv, right).wait_recv()

    def across_arrived(line, d, q):
        spot = piece(source(line, d), q)
        remote(spot, spot, ys.at[d - 1, line], yr.at[d - 1, line, q], right).wait_recv()

    def both_ways(d, q):
        @pl.when(has_right)
        def _():
            along(z, d, q, 0).start()

        @pl.when(has_left)
        def _():
            along(z, d, q, 1).start()

    for q in range(chunks):
        for d in range(1, ny):
            across(z, d, q).start()
        both_ways(0, q)
    for load in loads:
        load.start()

    for load in small_loads:
        load.wait()
    point = lax.broadcasted_iota(jnp.int32, (slab, batch), 1)
    wanted = lax.broadcasted_iota(jnp.int32, (slab, batch), 0) + place * slab
    here = [
        jnp.sum(
            jnp.where(point == wanted, coords_ref[d : d + 1, :], 0.0), axis=1, keepdims=True
        )
        for d in range(3)
    ]
    for j in range(blocks):
        lanes = slice(j * block, (j + 1) * block)
        distance = None
        for d in range(3):
            offset = centers_ref[d : d + 1, lanes] - here[d]
            distance = offset * offset if distance is None else distance + offset * offset
        coefficient = 1.0 / jnp.sqrt(distance + widths_ref[0:1, lanes])
        scaled_ref[j * slab : (j + 1) * slab, :] = coefficient * listed(sig_ref, 0, j)

    for q in range(EARLY):
        for d in range(1, ny):
            across_arrived(z, d, q)
            both_ways(d, q)

    total_rows = blocks * slab
    row = lax.broadcasted_iota(jnp.int32, (total_rows, blocks), 0)
    first = lax.broadcasted_iota(jnp.int32, (total_rows, blocks), 1) * slab
    expand = jnp.where((row >= first) & (row < first + slab), 1.0, 0.0).astype(bf16)
    screen = mask_ref[...].astype(f32).astype(bf16)
    spread = dot(dot(expand, screen).astype(bf16), expand, NT)
    row = lax.broadcasted_iota(jnp.int32, (total_rows, total_rows), 0)
    column = lax.broadcasted_iota(jnp.int32, (total_rows, total_rows), 1)
    spread_ref[...] = jnp.where(
        lax.rem(row, slab) == lax.rem(column, slab), spread, 0.0
    ).astype(bf16)
    for s in range(strips):
        for m in range(tile_blocks):
            flags_ref[s, m] = listed(domain_ref, s, t * tile_blocks + m)

    near = jnp.minimum(z, nz - 1 - z)

    def nearest(i):
        paired = z - (i + 1) // 2 if i % 2 else z + i // 2
        single = jnp.where(z < nz - 1 - z, i, nz - 1 - i)
        return jnp.where(i <= 2 * near, paired, single)

    order = [nearest(i) for i in range(nz)]

    row_start = pl.multiple_of((g * rows) % cols, rows)
    owner = (g * rows) // cols
    is_owner = owner == t
    in_column = owner % nc == c

    def share(line, d):
        src = source(line, d)

        @pl.when(is_owner)
        def _():
            for i, peer in enumerate(x_peers + [sibling]):
                remote(
                    all_ref.at[src, :, pl.ds(row_start, rows)],
                    rows_ref.at[src],
                    es.at[i],
                    er.at[src],
                    peer,
                ).start()

    def take_across(i):
        for d in range(1, ny):
            for q in range(EARLY if i == 0 else EARLY, chunks):
                across_arrived(order[i], d, q)
            share(order[i], d)

    def serve(step, q):
        for lane, line, here_, onward in (
            (0, z - step, z >= step, has_right),
            (1, z + step, z + step <= nz - 1, has_left),
        ):

            @pl.when(here_)
            def _():
                for d in range(ny if q < EARLY else 1):
                    along_arrived(line, d, q, lane)

                    @pl.when(onward)
                    def _():
                        along(line, d, q, lane).start()

                if q >= EARLY:
                    for d in range(1, ny):
                        across(line, d, q).start()

    def gathered(q):
        return all_ref[:, :, q * CHUNK : (q + 1) * CHUNK].reshape(grid_count * batch, CHUNK)

    def product(q, i):
        return dot(
            gathered(q), density_ref[i * block : (i + 1) * block, q * CHUNK : (q + 1) * CHUNK], NT
        )

    late = max(1, nz - 2)

    def multiply(q):
        if q >= EARLY:
            for i in range(late, nz):
                for d in range(1, ny):
                    across_arrived(order[i], d, q)
        if q == chunks - 1:
            return
        for i in range(row_blocks):
            lanes = slice(i * block, (i + 1) * block)
            if q == 0:
                acc_ref[:, lanes] = product(q, i)
            else:
                acc_ref[:, lanes] = acc_ref[:, lanes] + product(q, i)

    share(z, 0)
    for step in range(1, nz):
        last = step == nz - 1
        if last:
            density_load.wait()
        for q in range(chunks):
            serve(step, q)
            if last and q >= LAG:
                multiply(q - LAG)
        if step < late + 1 and step - 1 < late:
            take_across(step - 1)
        if not last:
            share(order[step], 0)
    if nz == 1:
        density_load.wait()
    for q in range(max(0, chunks - LAG) if nz > 1 else 0, chunks):
        multiply(q)

    def core_copy(i):
        return remote(part_ref.at[i, 1 - c], sibling_ref.at[i], cs.at[i], cr.at[i], sibling)

    def pair_copy(i, d):
        return remote(
            pair_ref.at[i, d - 1], peer_ref.at[i, d - 1], xs.at[i, d - 1], xr.at[i, d - 1],
            x_peers[d - 1],
        )

    def finish_product(i):
        lanes = slice(i * block, (i + 1) * block)
        value = product(chunks - 1, i)
        if chunks > 1:
            value = value + acc_ref[:, lanes]
        if slab % 8 == 0:
            split = value.reshape(grid_count, nc, nx, slab, block).astype(bf16)
            for e in range(nc):
                part_ref[i, e] = split[:, e]
        else:
            for n in range(grid_count):
                for e in range(nc):
                    for h in range(nx):
                        start = ((n * nc + e) * nx + h) * slab
                        part_ref[i, e, n, h] = value[start : start + slab].astype(bf16)
        core_copy(i).start()

    def exchange(i):
        core_copy(i).wait_recv()
        for d in range(1, nx):
            column = lax.rem(x + d, nx)

            @pl.loop(0, grid_count)
            def _(n):
                pair_ref[i, d - 1, n] = (
                    part_ref[i, c, n, column].astype(f32)
                    + sibling_ref[i, n, column].astype(f32)
                ).astype(bf16)

            pair_copy(i, d).start()

    for i in range(row_blocks):
        finish_product(i)
        if i:
            exchange(i - 1)
    exchange(row_blocks - 1)

    for i in range(late, nz):
        if i == nz - 1 and nz > 1:
            share(order[i], 0)
        for d in range(1, ny):
            share(order[i], d)

    own_rows = pltpu.make_async_copy(
        all_ref.at[:, :, pl.ds(row_start, rows)], rows_ref, local_sem
    )

    @pl.when(is_owner)
    def _():
        own_rows.start()

    far_order = [
        (order[i], d) for i in range(nz - 1, -1, -1) for d in range(ny) if i or d
    ]
    targets = [(line * ny + lax.rem(y + d, ny), n) for n, (line, d) in enumerate(far_order)]
    senders = [line * ny + lax.rem(y + ny - d, ny) for line, d in far_order]

    def return_copy(i, target, n):
        return remote(
            total_ref.at[i, target], back_ref.at[g, i], gs.at[i, n], gr.at[i, g], (target, t)
        )

    for i in range(row_blocks):
        for d in range(1, nx):
            pair_copy(i, d).wait_recv()

        @pl.loop(0, grid_count)
        def _(n):
            value = part_ref[i, c, n, x].astype(f32) + sibling_ref[i, n, x].astype(f32)
            for d in range(1, nx):
                value = value + peer_ref[i, d - 1, n].astype(f32)
            total_ref[i, n] = value.astype(bf16)

        for target, n in targets:
            return_copy(i, target, n).start()
        back_ref[g, i] = total_ref[i, g]

    @pl.when(jnp.logical_and(in_column, jnp.logical_not(is_owner)))
    def _():
        for src in range(grid_count):
            spot = rows_ref.at[src]
            pass_on = remote(spot, spot, es.at[nx - 1], er.at[src], sibling)
            pass_on.wait_recv()
            pass_on.start()

    core_load.wait()
    for sender in reversed(senders):
        for i in range(row_blocks):
            spot = back_ref.at[sender, i]
            remote(spot, spot, gs.at[i, 0], gr.at[i, sender], right).wait_recv()
    for j in range(blocks):
        span = slice(j * slab, (j + 1) * slab)
        weighted_ref[span, :] = scaled_ref[span, :] * back_ref[
            j // row_blocks, j % row_blocks
        ].astype(f32)
    weighted = weighted_ref[...].astype(bf16)

    tile_rows = tile_blocks * slab
    v_copies = []
    for n, tile in enumerate(tile_order):
        span = pl.ds(pl.multiple_of(tile * tile_rows, tile_rows), tile_rows)
        screened = dot(spread_ref[span, :], weighted).astype(bf16)
        potential = scaled_ref[span, :] * dot(screened, core_ref[...], NT)
        is_own = n == len(tile_order) - 1
        for m in range(tile_blocks):
            value = potential[m * slab : (m + 1) * slab, :].astype(bf16)
            if is_own:
                got_ref[place, m] = value
            else:
                pot_ref[n, m] = value
        if not is_own:
            copy = remote(
                pot_ref.at[n], got_ref.at[place], vs.at[n], vr.at[place], (g, tile)
            )
            copy.start()
            v_copies.append(copy)

    lmo_load.wait()
    places = [(tile % nc) * nx + tile // nc for tile in tile_order]
    for n in reversed(range(tile_count - 1)):
        spot = got_ref.at[places[n]]
        remote(spot, spot, vs.at[n], vr.at[places[n]], right).wait_recv()
    for i in range(tile_count):
        for m in range(tile_blocks):
            flat_ref[i * slab : (i + 1) * slab, m * block : (m + 1) * block] = got_ref[
                i, m
            ].astype(f32)

    w_copies = []
    own_total = None
    for n, tile in enumerate(tile_order):
        pieces = []
        for k in range(per_tile):
            s = tile * per_tile + k
            kept = jnp.concatenate(
                [
                    (flat_ref[:, m * block : (m + 1) * block] * flags_ref[s, m]).astype(bf16)
                    for m in range(tile_blocks)
                ],
                axis=1,
            )
            start = pl.multiple_of(s * strip_width, strip_width)
            pieces.append(dot(kept, lmo_ref[:, pl.ds(start, strip_width)]))
        value = pieces[0] if per_tile == 1 else jnp.concatenate(pieces, axis=1)
        if n < tile_count - 1:
            send_ref[n] = value.astype(bf16)
            copy = remote(send_ref.at[n], share_ref.at[t], ws.at[n], wr.at[t], (g, tile))
            copy.start()
            w_copies.append(copy)
        else:
            own_total = value
    for n in reversed(range(tile_count - 1)):
        tile = tile_order[n]
        spot = share_ref.at[tile]
        remote(spot, spot, ws.at[n], wr.at[tile], right).wait_recv()
        own_total = own_total + share_ref[tile].astype(f32)
    own_ref[...] = own_total.astype(bf16)
    f_copies = []
    for target, n in targets:
        copy = remote(own_ref, weights_ref.at[g], fs.at[n], fr.at[g], (target, t))
        copy.start()
        f_copies.append(copy)
    weights_ref[g] = own_ref[...]

    @pl.when(is_owner)
    def _():
        own_rows.wait()

    @pl.when(jnp.logical_not(in_column))
    def _():
        for src in range(grid_count):
            spot = rows_ref.at[src]
            remote(spot, spot, es.at[0], er.at[src], right).wait_recv()

    for sender in reversed(senders):
        spot = weights_ref.at[sender]
        remote(spot, spot, fs.at[0], fr.at[sender], right).wait_recv()
    out_ref[...] = dot(
        weights_ref[...].reshape(grid_count * batch, weights_ref.shape[2]),
        rows_ref[...].reshape(grid_count * batch, rows),
        TN,
    ).astype(bf16)

    for line in range(nz):
        for lane, sent in (
            (0, jnp.logical_and(has_right, line <= z)),
            (1, jnp.logical_and(has_left, line >= z)),
        ):

            @pl.when(sent)
            def _():
                spot = all_ref.at[0]
                remote(spot, spot, zs.at[lane, line], zr.at[0, 0, 0], right).wait_send()
                spot = all_ref.at[0, :, pl.ds(0, EARLY * CHUNK)]
                for d in range(1, ny):
                    remote(
                        spot, spot, ds_.at[lane, line, d - 1], zr.at[0, 0, 0], right
                    ).wait_send()

    for i in range(nz):
        width = cols if i == 0 else cols - EARLY * CHUNK
        spot = all_ref.at[0, :, pl.ds(0, width)]
        for d in range(1, ny):
            remote(spot, spot, ys.at[d - 1, order[i]], zr.at[0, 0, 0], right).wait_send()

    @pl.when(is_owner)
    def _():
        for i in range(nx):
            remote(rows_ref, rows_ref, es.at[i], er.at[0], right).wait_send()

    @pl.when(jnp.logical_and(in_column, jnp.logical_not(is_owner)))
    def _():
        remote(rows_ref, rows_ref, es.at[nx - 1], er.at[0], right).wait_send()

    for i in range(row_blocks):
        core_copy(i).wait_send()
        for d in range(1, nx):
            pair_copy(i, d).wait_send()
        for target, n in targets:
            return_copy(i, target, n).wait_send()
    for copy in v_copies + w_copies + f_copies:
        copy.wait_send()


def shards(
    point_values,
    sig_blocks,
    density,
    coulomb_core,
    screen_mask,
    ao_centers,
    ao_widths,
    point_coords,
    lmo_coeffs,
    domain_blocks,
):
    grid_count, tile_count = lax.axis_size("grid"), lax.axis_size("tile")
    nz, ny = grid_split(grid_count)
    nc, nx = 2, tile_count // 2
    rows, cols = density.shape
    batch = point_values.shape[0]
    block = coulomb_core.shape[0]
    total = ao_widths.shape[0]
    blocks = total // block
    slab = batch // tile_count
    strip = lmo_coeffs.shape[1] // tile_count
    tile_blocks, row_blocks, chunks = cols // block, rows // block, cols // CHUNK
    dma = pltpu.SemaphoreType.DMA
    smem = pl.BlockSpec(memory_space=pltpu.SMEM)
    vmem = pl.BlockSpec(memory_space=pltpu.VMEM)
    anywhere = pl.BlockSpec(memory_space=pl.ANY)
    side = max(1, ny - 1)
    return pl.pallas_call(
        functools.partial(kernel, nz, ny, nx),
        out_shape=jax.ShapeDtypeStruct((strip, rows), bf16),
        in_specs=[smem, smem, vmem] + [anywhere] * 7,
        out_specs=vmem,
        scratch_shapes=[
            pltpu.VMEM((grid_count, batch, cols), bf16),
            pltpu.VMEM((rows, cols), bf16),
            pltpu.VMEM((grid_count * batch, rows), f32),
            pltpu.VMEM((row_blocks, nc, grid_count, nx, slab, block), bf16),
            pltpu.VMEM((row_blocks, grid_count, nx, slab, block), bf16),
            pltpu.VMEM((row_blocks, max(1, nx - 1), grid_count, slab, block), bf16),
            pltpu.VMEM((row_blocks, max(1, nx - 1), grid_count, slab, block), bf16),
            pltpu.VMEM((row_blocks, grid_count, slab, block), bf16),
            pltpu.VMEM((grid_count, row_blocks, slab, block), bf16),
            pltpu.VMEM(coulomb_core.shape, bf16),
            pltpu.VMEM(screen_mask.shape, jnp.int32),
            pltpu.VMEM(ao_centers.shape, f32),
            pltpu.VMEM((1, total), f32),
            pltpu.VMEM(point_coords.shape, f32),
            pltpu.VMEM(lmo_coeffs.shape, bf16),
            pltpu.VMEM((blocks * slab, block), f32),
            pltpu.VMEM((blocks * slab, blocks * slab), bf16),
            pltpu.VMEM((blocks * slab, block), f32),
            pltpu.VMEM((tile_count - 1, tile_blocks, slab, block), bf16),
            pltpu.VMEM((tile_count, tile_blocks, slab, block), bf16),
            pltpu.VMEM((batch, cols), f32),
            pltpu.VMEM((tile_count - 1, batch, strip), bf16),
            pltpu.VMEM((tile_count, batch, strip), bf16),
            pltpu.VMEM((batch, strip), bf16),
            pltpu.VMEM((grid_count, batch, strip), bf16),
            pltpu.VMEM((grid_count, batch, rows), bf16),
            pltpu.SMEM((domain_blocks.shape[0], tile_blocks), f32),
            dma((2, nz)),
            dma((2, nz, chunks)),
            dma((2, nz, side)),
            dma((2, nz, side, EARLY)),
            dma((side, nz)),
            dma((side, nz, chunks)),
            dma((nx,)),
            dma((grid_count,)),
            dma,
            dma((7,)),
            dma((row_blocks,)),
            dma((row_blocks,)),
            dma((row_blocks, max(1, nx - 1))),
            dma((row_blocks, max(1, nx - 1))),
            dma((row_blocks, grid_count)),
            dma((row_blocks, grid_count)),
            dma((tile_count,)),
            dma((tile_count,)),
            dma((tile_count,)),
            dma((tile_count,)),
            dma((grid_count,)),
            dma((grid_count,)),
        ],
        compiler_params=pltpu.CompilerParams(
            collective_id=0, has_side_effects=True, vmem_limit_bytes=VMEM_LIMIT
        ),
    )(
        sig_blocks,
        domain_blocks,
        point_values,
        density,
        coulomb_core,
        screen_mask,
        ao_centers,
        ao_widths.reshape(1, total),
        point_coords,
        lmo_coeffs,
    )


def solution(mesh):
    in_specs = (
        P("grid", "tile"),
        P("grid", None),
        P("grid", "tile"),
        P(),
        P(),
        P(),
        P(),
        P(None, "grid"),
        P("tile", None),
        P(),
    )
    out_specs = P("tile", "grid")
    return jax.shard_map(shards, mesh=mesh, in_specs=in_specs, out_specs=out_specs, check_vma=False)
```

time: 75.9 us -> 64.3 us (0.85)
  Pallas kernels: 70.1 us -> 61.9 us
  matrix products: 3.61 us -> 0 us
  local copies, waits for them, and re-layouts: 1.27 us -> 2.3 us
    pallas_call x2 -> x1, Pallas kernels: 70.1 us -> 61.9 us  [shards(): pl.pallas_call(functools.partial(kernel, nz, ny, nx), out_shape=jax.Shape...]
    dot_general x3 -> x0, matrix products: 3.61 us -> none  [the longest x1 2.34 us: shards(): lax.dot_general(weights.reshape(grid_count * points, weights.shape[2]), r...]
    unnamed x15 -> x1, local copies, waits for them, and re-layouts: 0.16 us -> 2.3 us
    slice x1 -> x0, local copies, waits for them, and re-layouts: 1.03 us -> none
where the time goes in v1:
time: 64.3 us; the launch traced here: 64.2 us
  Pallas kernels  61.9 us (96%)
  local copies, waits for them, and re-layouts  2.3 us (4%)
    pallas_call x1, Pallas kernels, shards(): pl.pallas_call(functools.partial(kernel, nz, ny, nx), out_shape=jax.Shape...  61.9 us
    unnamed x1, local copies, waits for them, and re-layouts  2.3 us

profile of v1, /device:TPU:0, one launch (start us, length us, event | category | flops | bytes accessed | tf_op | source)
XLA Modules:
  0.0 64.2 jit_solution(17241823573710562567)
XLA Ops:
  0.0 61.9 %shard_map.100 = bf16[256,2048]{1,0:T(8,128)(2,1)} custom-call(s32[1,16]{1,0:T(1,128)} %sig_ref.1, s32[4,16]{1,0:T(4,128)} %domain_ref.1, bf16[32,4096]{1,0:T(8,128)(2,1)} %value_ref.1, bf16[2048,4096]{1,0:T(8,128)(2,1)} %density_hbm.1, bf16[512,512]{1,0:T(8,128)(2,1)} %core_hbm.1, s32[32,32]{1,0:T(8,128)} %mask_hbm.1, f32[3,16384]{1,0:T(4,128)} %centers_hbm.1, ...), custom_call_target="tpu_custom_call" | custom-call | tf_op jit(solution)/shard_map/pallas_call | solution.py:626
  61.9 2.3 %copy.12 = bf16[256,2048]{1,0:T(8,128)(2,1)} copy(bf16[256,2048]{1,0:T(8,128)(2,1)} %shard_map.100) | data formatting | bytes 2097152

commit v2 on v1

v2 whole, which is shorter than its diff:
```python
import functools
import math

import jax
import jax.numpy as jnp
from jax import lax
from jax.experimental import pallas as pl
from jax.experimental.pallas import tpu as pltpu
from jax.sharding import PartitionSpec as P

MESH = pl.DeviceIdType.MESH
VMEM_LIMIT = 48 * 1024 * 1024
CHUNK = 512
LAG = 3
f32 = jnp.float32
bf16 = jnp.bfloat16
NT = (((1,), (1,)), ((), ()))
TN = (((0,), (0,)), ((), ()))


def grid_split(grid_count):
    inner = max(1, math.isqrt(max(1, grid_count // 2)))
    while grid_count % inner:
        inner -= 1
    return grid_count // inner, inner


def column_cuts(cols):
    early = max(128, cols * 5 // 32 // 128 * 128)
    cuts = [(start, min(CHUNK, cols - early - start)) for start in range(0, cols - early, CHUNK)]
    return cuts + [(cols - early, early)]


def remote(src, dst, send_sem, recv_sem, device):
    return pltpu.make_async_remote_copy(
        src_ref=src,
        dst_ref=dst,
        send_sem=send_sem,
        recv_sem=recv_sem,
        device_id=device,
        device_id_type=MESH,
    )


def listed(table_ref, row, block_id):
    flag = jnp.float32(0.0)
    for i in range(table_ref.shape[1]):
        flag = jnp.where(table_ref[row, i] == block_id, jnp.float32(1.0), flag)
    return flag


def dot(a, b, dims=(((1,), (0,)), ((), ()))):
    return lax.dot_general(a, b, dims, preferred_element_type=f32)


def kernel(
    nz,
    ny,
    nx,
    sig_ref,
    domain_ref,
    value_ref,
    density_hbm,
    core_hbm,
    mask_hbm,
    centers_hbm,
    widths_hbm,
    coords_hbm,
    lmo_hbm,
    out_ref,
    all_ref,
    density_ref,
    acc_ref,
    part_ref,
    sibling_ref,
    pair_ref,
    peer_ref,
    total_ref,
    back_ref,
    core_ref,
    mask_ref,
    centers_ref,
    widths_ref,
    coords_ref,
    lmo_ref,
    scaled_ref,
    spread_ref,
    weighted_ref,
    pot_ref,
    got_ref,
    flat_ref,
    send_ref,
    share_ref,
    own_ref,
    weights_ref,
    rows_ref,
    flags_ref,
    half_ref,
    product_ref,
    zs,
    zr,
    ds_,
    dr,
    ys,
    ye,
    yl,
    yt,
    es,
    er,
    local_sem,
    load_sem,
    cs,
    cr,
    xs,
    xr,
    gs,
    gr,
    vs,
    vr,
    ws,
    wr,
    fs,
    fr,
):
    grid_count, tile_count, nc = nz * ny, nx * 2, 2
    batch, cols = value_ref.shape
    rows = density_ref.shape[0]
    block = core_ref.shape[0]
    blocks = mask_ref.shape[0]
    slab = batch // tile_count
    tile_blocks = cols // block
    row_blocks = rows // block
    cuts = column_cuts(cols)
    chunks = len(cuts)
    early = cuts[-1][1]
    tip = chunks - 1
    strips = domain_ref.shape[0]
    strip_width = lmo_ref.shape[1] // strips
    per_tile = strips // tile_count

    g, t = lax.axis_index("grid"), lax.axis_index("tile")
    z, y = g // ny, g % ny
    x, c = t // nc, t % nc
    place = c * nx + x
    has_left, has_right = z > 0, z < nz - 1
    left = (lax.rem(z + nz - 1, nz) * ny + y, t)
    right = (lax.rem(z + 1, nz) * ny + y, t)
    y_peers = [(z * ny + lax.rem(y + d, ny), t) for d in range(1, ny)]
    x_peers = [(g, lax.rem(x + d, nx) * nc + c) for d in range(1, nx)]
    sibling = (g, x * nc + (1 - c))
    far_tiles = [
        lax.rem(x + d, nx) * nc + (c if e == 0 else 1 - c) for d in range(1, nx) for e in range(nc)
    ]
    tile_order = far_tiles + [x * nc + (1 - c), t]

    loads = [
        pltpu.make_async_copy(src, dst, load_sem.at[i])
        for i, (src, dst) in enumerate(
            [
                (coords_hbm, coords_ref),
                (widths_hbm, widths_ref),
                (centers_hbm, centers_ref),
                (mask_hbm, mask_ref),
                (core_hbm, core_ref),
                (density_hbm, density_ref),
                (lmo_hbm, lmo_ref),
            ]
        )
    ]
    small_loads, core_load, density_load, lmo_load = loads[:4], loads[4], loads[5], loads[6]

    barrier = pltpu.get_barrier_semaphore()

    def hello(device):
        pl.semaphore_signal(barrier, inc=1, device_id=device, device_id_type=MESH)

    @pl.when(has_left)
    def _():
        hello(left)

    @pl.when(has_right)
    def _():
        hello(right)

    for peer in y_peers + [(g, tile) for tile in tile_order[:-1]]:
        hello(peer)

    for m in range(tile_blocks):
        lanes = slice(m * block, (m + 1) * block)
        flag = listed(sig_ref, 0, t * tile_blocks + m)
        all_ref[g, :, lanes] = (value_ref[:, lanes].astype(f32) * flag).astype(bf16)

    neighbours = (
        ny - 1 + tile_count - 1 + jnp.where(has_left, 1, 0) + jnp.where(has_right, 1, 0)
    )
    pl.semaphore_wait(barrier, neighbours)

    def source(line, d):
        return line * ny + lax.rem(y + ny - d, ny)

    def piece(src, q):
        return all_ref.at[src, :, pl.ds(*cuts[q])]

    def z_sems(lane, line, d, q):
        slot = line - lane
        if d == 0:
            return zs.at[lane, line], zr.at[slot, q]
        return ds_.at[lane, line, d - 1], dr.at[slot, d - 1]

    def along(line, d, q, lane):
        spot = piece(source(line, d), q)
        send, recv = z_sems(lane, line, d, q)
        return remote(spot, spot, send, recv, left if lane else right)

    def across(line, d, q, sems):
        spot = piece(source(line, 0), q)
        return remote(spot, spot, *sems, y_peers[d - 1])

    def along_arrived(line, d, q, lane):
        spot = piece(source(line, d), q)
        send, recv = z_sems(lane, line, d, q)
        remote(spot, spot, send, recv, right).wait_recv()

    def arrived(spot, recv):
        remote(spot, spot, ys.at[0, 0], recv, right).wait_recv()

    def both_ways(d, q):
        @pl.when(has_right)
        def _():
            along(z, d, q, 0).start()

        @pl.when(has_left)
        def _():
            along(z, d, q, 1).start()

    half = nz // 2

    def send_across(i, line, q):
        if q != tip:
            for d in range(1, ny):
                recv = ye.at[d - 1, i] if i < half else yl.at[d - 1, q]
                across(line, d, q, (ys.at[d - 1, i], recv)).start()

    for d in range(1, ny):
        across(z, d, tip, (ys.at[d - 1, nz], yt.at[d - 1])).start()
    for q in range(chunks):
        both_ways(0, q)
        send_across(0, z, q)
    for load in loads:
        load.start()

    for load in small_loads:
        load.wait()
    point = lax.broadcasted_iota(jnp.int32, (slab, batch), 1)
    wanted = lax.broadcasted_iota(jnp.int32, (slab, batch), 0) + place * slab
    here = [
        jnp.sum(
            jnp.where(point == wanted, coords_ref[d : d + 1, :], 0.0), axis=1, keepdims=True
        )
        for d in range(3)
    ]
    for j in range(blocks):
        lanes = slice(j * block, (j + 1) * block)
        distance = None
        for d in range(3):
            offset = centers_ref[d : d + 1, lanes] - here[d]
            distance = offset * offset if distance is None else distance + offset * offset
        coefficient = 1.0 / jnp.sqrt(distance + widths_ref[0:1, lanes])
        scaled_ref[j * slab : (j + 1) * slab, :] = coefficient * listed(sig_ref, 0, j)

    for d in range(1, ny):
        arrived(piece(source(z, d), tip), yt.at[d - 1])
        both_ways(d, tip)

    total_rows = blocks * slab
    row = lax.broadcasted_iota(jnp.int32, (total_rows, blocks), 0)
    first = lax.broadcasted_iota(jnp.int32, (total_rows, blocks), 1) * slab
    expand = jnp.where((row >= first) & (row < first + slab), 1.0, 0.0).astype(bf16)
    screen = mask_ref[...].astype(f32).astype(bf16)
    spread = dot(dot(expand, screen).astype(bf16), expand, NT)
    row = lax.broadcasted_iota(jnp.int32, (total_rows, total_rows), 0)
    column = lax.broadcasted_iota(jnp.int32, (total_rows, total_rows), 1)
    spread_ref[...] = jnp.where(
        lax.rem(row, slab) == lax.rem(column, slab), spread, 0.0
    ).astype(bf16)
    for s in range(strips):
        for m in range(tile_blocks):
            flags_ref[s, m] = listed(domain_ref, s, t * tile_blocks + m)

    near = jnp.minimum(z, nz - 1 - z)

    def nearest(i):
        step = (i + 1) // 2 if i % 2 else -(i // 2)
        low = z < nz - 1 - z
        paired = jnp.where(low, z + step, z - step)
        single = jnp.where(low, i, nz - 1 - i)
        return jnp.where(i <= 2 * near, paired, single)

    order = [nearest(i) for i in range(nz)]

    row_start = pl.multiple_of((g * rows) % cols, rows)
    owner = (g * rows) // cols
    is_owner = owner == t
    in_column = owner % nc == c

    def share(line, d):
        src = source(line, d)

        @pl.when(is_owner)
        def _():
            for i, peer in enumerate(x_peers + [sibling]):
                remote(
                    all_ref.at[src, :, pl.ds(row_start, rows)],
                    rows_ref.at[src],
                    es.at[i],
                    er.at[src],
                    peer,
                ).start()

    def take_across(i):
        for d in range(1, ny):
            arrived(all_ref.at[0, :, pl.ds(0, cols - early)], ye.at[d - 1, i])
            share(order[i], d)

    def serve(step, q, sources):
        for lane, line, here_, onward in (
            (0, z - step, z >= step, has_right),
            (1, z + step, z + step <= nz - 1, has_left),
        ):

            @pl.when(here_)
            def _():
                for d in sources:
                    along_arrived(line, d, q, lane)

                    @pl.when(onward)
                    def _():
                        along(line, d, q, lane).start()

    members = [source(order[i], d) for i in range(nz) for d in range(ny)]
    size = half * ny
    groups = (members[:size], members[size:])

    def gathered(group, start, width):
        return jnp.concatenate(
            [all_ref[src, :, start : start + width] for src in groups[group]], axis=0
        )

    def multiply(q):
        start, width = cuts[q]
        if q != tip:
            for d in range(1, ny):
                arrived(all_ref.at[pl.ds(0, nz - half), :, pl.ds(start, width)], yl.at[d - 1, q])
        values = gathered(1, start, width)
        for i in range(row_blocks):
            lanes = slice(i * block, (i + 1) * block)
            value = dot(values, density_ref[lanes, start : start + width], NT)
            if q:
                value = acc_ref[:, lanes] + value
            if q == tip:
                store_part(1, i, value)
                core_copy(1, i).start()
                if i > 0:
                    exchange(1, i - 1)
            else:
                acc_ref[:, lanes] = value

    def store_part(group, i, value):
        if slab % 8 == 0:
            split = value.reshape(size, nc, nx, slab, block).astype(bf16)
            for e in range(nc):
                for h in range(nx):
                    part_ref[group, i, e, h] = split[:, e, h]
        else:
            for n in range(size):
                for e in range(nc):
                    for h in range(nx):
                        first = ((n * nc + e) * nx + h) * slab
                        part_ref[group, i, e, h, n] = value[first : first + slab].astype(bf16)

    def core_copy(group, i):
        return remote(
            part_ref.at[group, i, 1 - c], sibling_ref.at[group, i], cs, cr.at[group, i], sibling
        )

    def pair_copy(group, i, d):
        return remote(
            pair_ref.at[group, i, d - 1],
            peer_ref.at[group, i, d - 1],
            xs.at[d - 1],
            xr.at[group, i, d - 1],
            x_peers[d - 1],
        )

    def exchange(group, i):
        core_copy(group, i).wait_recv()
        for d in range(1, nx):
            column = lax.rem(x + d, nx)
            pair_ref[group, i, d - 1] = (
                part_ref[group, i, c, column].astype(f32)
                + sibling_ref[group, i, column].astype(f32)
            ).astype(bf16)
            pair_copy(group, i, d).start()

    def collect(group, i):
        for d in range(1, nx):
            pair_copy(group, i, d).wait_recv()
        value = part_ref[group, i, c, x].astype(f32) + sibling_ref[group, i, x].astype(f32)
        for d in range(1, nx):
            value = value + peer_ref[group, i, d - 1].astype(f32)
        total_ref[group, i] = value.astype(bf16)
        for n in reversed(range(size)):
            if group or n:
                remote(
                    total_ref.at[group, i, n], back_ref.at[g, i], gs, gr, (groups[group][n], t)
                ).start()
            else:
                back_ref[g, i] = total_ref[group, i, n]

    def part_product(i, late_half):
        middle = cols // 2
        lanes = slice(middle, cols) if late_half else slice(0, middle)
        rows_here = slice(i * block, (i + 1) * block)
        value = dot(
            gathered(0, lanes.start, middle), density_ref[rows_here, lanes], NT
        )
        if not late_half:
            half_ref[...] = value
            return
        store_part(0, i, half_ref[...] + value)
        core_copy(0, i).start()
        if i > 0:
            exchange(0, i - 1)

    def begin():
        density_load.wait()
        for i in range(1, half):
            take_across(i)

    items = [begin]
    for i in range(row_blocks):
        items += [functools.partial(part_product, i, e) for e in range(2)]
    after = [functools.partial(exchange, 0, row_blocks - 1)]
    after += [functools.partial(collect, 0, i) for i in range(row_blocks)]

    def pump(work, count=1):
        for _ in range(min(count, len(work))):
            work.pop(0)()

    done = 0
    share(z, 0)
    for step in range(1, nz):
        for q in range(chunks):
            serve(step, q, (0,))
            send_across(step, order[step], q)
            if (step, q) == (half, chunks // 2 - 1):
                pump(items)
            if (step, q) >= (half, chunks // 2 - 1):
                pump(items)
            if step == nz - 1 and q >= LAG:
                pump(items, len(items))
                multiply(done)
                done += 1
                if q > LAG:
                    pump(after)
        serve(step, tip, range(1, ny))
        if step == 1:
            take_across(0)
        if step < nz - 1:
            share(order[step], 0)
    pump(items, len(items))
    while done < tip:
        multiply(done)
        done += 1
        pump(after)
    pump(after, len(after))
    multiply(tip)
    exchange(1, row_blocks - 1)
    for i in range(row_blocks):
        collect(1, i)

    for i in range(half, nz):
        if i == nz - 1:
            share(order[i], 0)
        for d in range(1, ny):
            share(order[i], d)

    own_rows = pltpu.make_async_copy(
        all_ref.at[:, :, pl.ds(row_start, rows)], rows_ref, local_sem
    )

    @pl.when(is_owner)
    def _():
        own_rows.start()

    core_load.wait()
    def wait_all(spot, recv):
        remote(spot, spot, gs, recv, right).wait_recv()

    wait_all(back_ref.at[pl.ds(0, grid_count - 1)], gr)
    for j in range(blocks):
        span = slice(j * slab, (j + 1) * slab)
        weighted_ref[span, :] = scaled_ref[span, :] * back_ref[
            j // row_blocks, j % row_blocks
        ].astype(f32)
    weighted = weighted_ref[...].astype(bf16)

    tile_rows = tile_blocks * slab
    for n, tile in enumerate(tile_order):
        span = pl.ds(pl.multiple_of(tile * tile_rows, tile_rows), tile_rows)
        screened = dot(spread_ref[span, :], weighted).astype(bf16)
        potential = scaled_ref[span, :] * dot(screened, core_ref[...], NT)
        is_own = n == len(tile_order) - 1
        for m in range(tile_blocks):
            value = potential[m * slab : (m + 1) * slab, :].astype(bf16)
            if is_own:
                got_ref[place, m] = value
            else:
                pot_ref[n, m] = value
        if not is_own:
            remote(
                pot_ref.at[n], got_ref.at[place], vs, vr, (g, tile)
            ).start()

    lmo_load.wait()
    wait_all(got_ref.at[pl.ds(0, tile_count - 1)], vr)
    for i in range(tile_count):
        for m in range(tile_blocks):
            flat_ref[i * slab : (i + 1) * slab, m * block : (m + 1) * block] = got_ref[
                i, m
            ].astype(f32)

    own_total = None
    group_width = nc * per_tile * strip_width
    for n, (d, tiles) in enumerate(
        [(d, tile_order[2 * d - 2 : 2 * d]) for d in range(1, nx)] + [(0, tile_order[-2:])]
    ):
        plane = lax.rem(x + d, nx)
        kept = jnp.concatenate(
            [
                jnp.concatenate(
                    [
                        (
                            flat_ref[:, m * block : (m + 1) * block]
                            * flags_ref[plane * nc * per_tile + k, m]
                        ).astype(bf16)
                        for m in range(tile_blocks)
                    ],
                    axis=1,
                )
                for k in range(nc * per_tile)
            ],
            axis=0,
        )
        start = pl.multiple_of(plane * group_width, group_width)
        values = dot(kept, lmo_ref[:, pl.ds(start, group_width)])
        pieces = []
        for e in range(nc):
            parts = []
            for k in range(e * per_tile, (e + 1) * per_tile):
                parts.append(
                    values[
                        k * batch : (k + 1) * batch, k * strip_width : (k + 1) * strip_width
                    ]
                )
            pieces.append(parts[0] if per_tile == 1 else jnp.concatenate(parts, axis=1))
        for e in range(nc):
            product_ref[n, e] = pieces[e]
        for k, tile in enumerate(tiles):
            index = n * nc + k
            chosen = product_ref[n, lax.rem(tile, nc)]
            if index < tile_count - 1:
                send_ref[index] = chosen.astype(bf16)
                remote(send_ref.at[index], share_ref.at[t], ws, wr, (g, tile)).start()
            else:
                own_total = chosen
    wait_all(share_ref.at[pl.ds(0, tile_count - 1)], wr)
    for tile in tile_order[:-1]:
        own_total = own_total + share_ref[tile].astype(f32)
    own_ref[...] = own_total.astype(bf16)
    for target in reversed(members[1:]):
        remote(own_ref, weights_ref.at[g], fs, fr, (target, t)).start()
    weights_ref[g] = own_ref[...]

    @pl.when(jnp.logical_and(in_column, jnp.logical_not(is_owner)))
    def _():
        for src in range(grid_count):
            spot = rows_ref.at[src]
            pass_on = remote(spot, spot, es.at[nx - 1], er.at[src], sibling)
            pass_on.wait_recv()
            pass_on.start()

    @pl.when(is_owner)
    def _():
        own_rows.wait()

    @pl.when(jnp.logical_not(in_column))
    def _():
        for src in range(grid_count):
            spot = rows_ref.at[src]
            remote(spot, spot, es.at[0], er.at[src], right).wait_recv()

    wait_all(weights_ref.at[pl.ds(0, grid_count - 1)], fr)
    out_ref[...] = dot(
        weights_ref[...].reshape(grid_count * batch, weights_ref.shape[2]),
        rows_ref[...].reshape(grid_count * batch, rows),
        TN,
    ).astype(bf16)

    def drain(ref, sem):
        remote(ref, ref, sem, fr, right).wait_send()

    for line in range(nz):
        for lane, sent in (
            (0, jnp.logical_and(has_right, line <= z)),
            (1, jnp.logical_and(has_left, line >= z)),
        ):

            @pl.when(sent)
            def _():
                drain(all_ref.at[0], zs.at[lane, line])
                for d in range(1, ny):
                    drain(all_ref.at[0, :, pl.ds(cols - early, early)], ds_.at[lane, line, d - 1])

    for d in range(1, ny):
        for i in range(nz):
            drain(all_ref.at[0, :, pl.ds(0, cols - early)], ys.at[d - 1, i])
        drain(all_ref.at[0, :, pl.ds(0, early)], ys.at[d - 1, nz])

    @pl.when(is_owner)
    def _():
        for i in range(nx):
            drain(rows_ref, es.at[i])

    @pl.when(jnp.logical_and(in_column, jnp.logical_not(is_owner)))
    def _():
        drain(rows_ref, es.at[nx - 1])

    drain(sibling_ref, cs)
    for d in range(1, nx):
        drain(pair_ref.at[:, :, d - 1], xs.at[d - 1])
    drain(back_ref.at[pl.ds(0, grid_count - 1)], gs)
    drain(pot_ref, vs)
    drain(send_ref, ws)
    drain(weights_ref.at[pl.ds(0, grid_count - 1)], fs)


def shards(
    point_values,
    sig_blocks,
    density,
    coulomb_core,
    screen_mask,
    ao_centers,
    ao_widths,
    point_coords,
    lmo_coeffs,
    domain_blocks,
):
    grid_count, tile_count = lax.axis_size("grid"), lax.axis_size("tile")
    nz, ny = grid_split(grid_count)
    nc, nx = 2, tile_count // 2
    rows, cols = density.shape
    batch = point_values.shape[0]
    block = coulomb_core.shape[0]
    total = ao_widths.shape[0]
    blocks = total // block
    slab = batch // tile_count
    strip = lmo_coeffs.shape[1] // tile_count
    tile_blocks, row_blocks, chunks = cols // block, rows // block, len(column_cuts(cols))
    dma = pltpu.SemaphoreType.DMA
    smem = pl.BlockSpec(memory_space=pltpu.SMEM)
    vmem = pl.BlockSpec(memory_space=pltpu.VMEM)
    anywhere = pl.BlockSpec(memory_space=pltpu.HBM)
    side = max(1, ny - 1)
    size = nz // 2 * ny
    return pl.pallas_call(
        functools.partial(kernel, nz, ny, nx),
        out_shape=jax.ShapeDtypeStruct((strip, rows), bf16),
        in_specs=[smem, smem, vmem] + [anywhere] * 7,
        out_specs=vmem,
        scratch_shapes=[
            pltpu.VMEM((grid_count, batch, cols), bf16),
            pltpu.VMEM((rows, cols), bf16),
            pltpu.VMEM((size * batch, rows), f32),
            pltpu.VMEM((2, row_blocks, nc, nx, size, slab, block), bf16),
            pltpu.VMEM((2, row_blocks, nx, size, slab, block), bf16),
            pltpu.VMEM((2, row_blocks, max(1, nx - 1), size, slab, block), bf16),
            pltpu.VMEM((2, row_blocks, max(1, nx - 1), size, slab, block), bf16),
            pltpu.VMEM((2, row_blocks, size, slab, block), bf16),
            pltpu.VMEM((grid_count, row_blocks, slab, block), bf16),
            pltpu.VMEM(coulomb_core.shape, bf16),
            pltpu.VMEM(screen_mask.shape, jnp.int32),
            pltpu.VMEM(ao_centers.shape, f32),
            pltpu.VMEM((1, total), f32),
            pltpu.VMEM(point_coords.shape, f32),
            pltpu.VMEM(lmo_coeffs.shape, bf16),
            pltpu.VMEM((blocks * slab, block), f32),
            pltpu.VMEM((blocks * slab, blocks * slab), bf16),
            pltpu.VMEM((blocks * slab, block), f32),
            pltpu.VMEM((tile_count - 1, tile_blocks, slab, block), bf16),
            pltpu.VMEM((tile_count, tile_blocks, slab, block), bf16),
            pltpu.VMEM((batch, cols), f32),
            pltpu.VMEM((tile_count - 1, batch, strip), bf16),
            pltpu.VMEM((tile_count, batch, strip), bf16),
            pltpu.VMEM((batch, strip), bf16),
            pltpu.VMEM((grid_count, batch, strip), bf16),
            pltpu.VMEM((grid_count, batch, rows), bf16),
            pltpu.SMEM((domain_blocks.shape[0], tile_blocks), f32),
            pltpu.VMEM((size * batch, block), f32),
            pltpu.VMEM((nx, nc, batch, strip), f32),
            dma((2, nz)),
            dma((nz - 1, chunks)),
            dma((2, nz, side)),
            dma((nz - 1, side)),
            dma((side, nz + 1)),
            dma((side, nz // 2)),
            dma((side, chunks - 1)),
            dma((side,)),
            dma((nx,)),
            dma((grid_count,)),
            dma,
            dma((7,)),
            dma,
            dma((2, row_blocks)),
            dma((max(1, nx - 1),)),
            dma((2, row_blocks, max(1, nx - 1))),
            dma,
            dma,
            dma,
            dma,
            dma,
            dma,
            dma,
            dma,
        ],
        compiler_params=pltpu.CompilerParams(
            collective_id=0, has_side_effects=True, vmem_limit_bytes=VMEM_LIMIT
        ),
    )(
        *[
            pltpu.with_memory_space_constraint(operand, pltpu.HBM)
            for operand in (
                sig_blocks,
                domain_blocks,
                point_values,
                density,
                coulomb_core,
                screen_mask,
                ao_centers,
                ao_widths.reshape(1, total),
                point_coords,
                lmo_coeffs,
            )
        ]
    )


def solution(mesh):
    in_specs = (
        P("grid", "tile"),
        P("grid", None),
        P("grid", "tile"),
        P(),
        P(),
        P(),
        P(),
        P(None, "grid"),
        P("tile", None),
        P(),
    )
    out_specs = P("tile", "grid")
    return jax.shard_map(shards, mesh=mesh, in_specs=in_specs, out_specs=out_specs, check_vma=False)
```

time: 64.3 us -> 57.4 us (0.89)
  Pallas kernels: 61.9 us -> 56.2 us
  local copies, waits for them, and re-layouts: 2.3 us -> 0.97 us
    pallas_call x1, Pallas kernels: 61.9 us -> 56.2 us  [shards(): pl.pallas_call(functools.partial(kernel, nz, ny, nx), out_shape=jax.Shape...]
    unnamed x1, local copies, waits for them, and re-layouts: 2.3 us -> 0.97 us
where the time goes in v2:
time: 57.4 us; the launch traced here: 57.2 us
  Pallas kernels  56.2 us (98%)
  local copies, waits for them, and re-layouts  0.97 us (2%)
    pallas_call x1, Pallas kernels, shards(): pl.pallas_call(functools.partial(kernel, nz, ny, nx), out_shape=jax.Shape...  56.2 us

profile of v2, /device:TPU:0, one launch (start us, length us, event | category | flops | bytes accessed | tf_op | source)
XLA Modules:
  0.0 57.2 jit_solution(9071416324503093443)
XLA Ops:
  0.0 56.2 %shard_map.100 = bf16[256,2048]{1,0:T(8,128)(2,1)S(1)} custom-call(s32[1,16]{1,0:T(1,128)} %sig_ref.1, s32[4,16]{1,0:T(4,128)} %domain_ref.1, bf16[32,4096]{1,0:T(8,128)(2,1)} %value_ref.1, bf16[2048,4096]{1,0:T(8,128)(2,1)} %density_hbm.1, bf16[512,512]{1,0:T(8,128)(2,1)} %core_hbm.1, s32[32,32]{1,0:T(8,128)} %mask_hbm.1, f32[3,16384]{1,0:T(4,128)} %centers_hbm.1, ...), custom_call_target="tpu_custom_call" | custom-call | tf_op jit(solution)/shard_map/pallas_call | solution.py:677
  56.2 1.0 %copy.12 = bf16[256,2048]{1,0:T(8,128)(2,1)} copy(bf16[256,2048]{1,0:T(8,128)(2,1)S(1)} %shard_map.100) | data formatting | bytes 2097152

commit v3 on v2

--- a/solution.py
+++ b/solution.py
@@ -11,7 +11,7 @@
 MESH = pl.DeviceIdType.MESH
 VMEM_LIMIT = 48 * 1024 * 1024
 CHUNK = 512
-LAG = 3
+FILL = 128
 f32 = jnp.float32
 bf16 = jnp.bfloat16
 NT = (((1,), (1,)), ((), ()))
@@ -26,7 +26,7 @@
 
 
 def column_cuts(cols):
-    early = max(128, cols * 5 // 32 // 128 * 128)
+    early = max(128, cols * 4 // 32 // 128 * 128)
     cuts = [(start, min(CHUNK, cols - early - start)) for start in range(0, cols - early, CHUNK)]
     return cuts + [(cols - early, early)]
 
@@ -57,9 +57,9 @@
     nz,
     ny,
     nx,
-    sig_ref,
-    domain_ref,
-    value_ref,
+    sig_hbm,
+    domain_hbm,
+    value_hbm,
     density_hbm,
     core_hbm,
     mask_hbm,
@@ -68,8 +68,12 @@
     coords_hbm,
     lmo_hbm,
     out_ref,
+    sig_ref,
+    domain_ref,
+    value_ref,
     all_ref,
-    density_ref,
+    stage_ref,
+    turned_ref,
     acc_ref,
     part_ref,
     sibling_ref,
@@ -95,7 +99,6 @@
     weights_ref,
     rows_ref,
     flags_ref,
-    half_ref,
     product_ref,
     zs,
     zr,
@@ -124,7 +127,7 @@
 ):
     grid_count, tile_count, nc = nz * ny, nx * 2, 2
     batch, cols = value_ref.shape
-    rows = density_ref.shape[0]
+    rows = turned_ref.shape[1]
     block = core_ref.shape[0]
     blocks = mask_ref.shape[0]
     slab = batch // tile_count
@@ -153,21 +156,35 @@
     ]
     tile_order = far_tiles + [x * nc + (1 - c), t]
 
-    loads = [
+    small_loads = [
         pltpu.make_async_copy(src, dst, load_sem.at[i])
         for i, (src, dst) in enumerate(
             [
+                (sig_hbm, sig_ref),
+                (value_hbm, value_ref),
+                (domain_hbm, domain_ref),
                 (coords_hbm, coords_ref),
                 (widths_hbm, widths_ref),
                 (centers_hbm, centers_ref),
                 (mask_hbm, mask_ref),
                 (core_hbm, core_ref),
-                (density_hbm, density_ref),
                 (lmo_hbm, lmo_ref),
             ]
         )
     ]
-    small_loads, core_load, density_load, lmo_load = loads[:4], loads[4], loads[5], loads[6]
+    core_load, lmo_load = small_loads[7:]
+    first_loads, small_loads = small_loads[:2], small_loads[2:7]
+
+    def stage_load(i):
+        return pltpu.make_async_copy(
+            density_hbm.at[pl.ds(i * block, block)], stage_ref.at[i % 2], load_sem.at[9 + i % 2]
+        )
+
+    for load in first_loads + small_loads:
+        load.start()
+    for i in range(min(2, row_blocks)):
+        stage_load(i).start()
+    core_load.start()
 
     barrier = pltpu.get_barrier_semaphore()
 
@@ -185,6 +202,8 @@
     for peer in y_peers + [(g, tile) for tile in tile_order[:-1]]:
         hello(peer)
 
+    for load in first_loads:
+        load.wait()
     for m in range(tile_blocks):
         lanes = slice(m * block, (m + 1) * block)
         flag = listed(sig_ref, 0, t * tile_blocks + m)
@@ -238,7 +257,7 @@
     def send_across(i, line, q):
         if q != tip:
             for d in range(1, ny):
-                recv = ye.at[d - 1, i] if i < half else yl.at[d - 1, q]
+                recv = ye.at[d - 1, i] if i < nz - 1 else yl.at[d - 1, q]
                 across(line, d, q, (ys.at[d - 1, i], recv)).start()
 
     for d in range(1, ny):
@@ -246,8 +265,22 @@
     for q in range(chunks):
         both_ways(0, q)
         send_across(0, z, q)
-    for load in loads:
-        load.start()
+    def turn(i, k):
+        if k == 0:
+            stage_load(i).wait()
+        lanes = slice(k * block, (k + 1) * block)
+        turned_ref[lanes, i * block : (i + 1) * block] = stage_ref[i % 2, :, lanes].T
+        if k == tile_blocks - 1:
+            if i + 2 < row_blocks:
+                stage_load(i + 2).start()
+            if i == row_blocks - 1:
+                lmo_load.start()
+
+    turns = [functools.partial(turn, i, k) for i in range(row_blocks) for k in range(tile_blocks)]
+
+    def pump(work, count=1):
+        for _ in range(min(count, len(work))):
+            work.pop(0)()
 
     for load in small_loads:
         load.wait()
@@ -268,6 +301,7 @@
         coefficient = 1.0 / jnp.sqrt(distance + widths_ref[0:1, lanes])
         scaled_ref[j * slab : (j + 1) * slab, :] = coefficient * listed(sig_ref, 0, j)
 
+    pump(turns, tile_blocks)
     for d in range(1, ny):
         arrived(piece(source(z, d), tip), yt.at[d - 1])
         both_ways(d, tip)
@@ -338,152 +372,157 @@
                         along(line, d, q, lane).start()
 
     members = [source(order[i], d) for i in range(nz) for d in range(ny)]
-    size = half * ny
-    groups = (members[:size], members[size:])
+    lines = [list(range(half))] + [[i] for i in range(half, nz)]
+    spans = [(group[0] * ny, (group[-1] + 1) * ny) for group in lines]
+    final = len(lines) - 1
 
     def gathered(group, start, width):
+        first, stop = spans[group]
+        sources = members[first:stop]
+        if group != final:
+            sources = sources * max(1, FILL // ((stop - first) * batch))
         return jnp.concatenate(
-            [all_ref[src, :, start : start + width] for src in groups[group]], axis=0
+            [all_ref[src, :, start : start + width] for src in sources], axis=0
         )
 
     def multiply(q):
         start, width = cuts[q]
         if q != tip:
             for d in range(1, ny):
-                arrived(all_ref.at[pl.ds(0, nz - half), :, pl.ds(start, width)], yl.at[d - 1, q])
-        values = gathered(1, start, width)
+                arrived(piece(0, q), yl.at[d - 1, q])
+        values = gathered(final, start, width)
         for i in range(row_blocks):
             lanes = slice(i * block, (i + 1) * block)
-            value = dot(values, density_ref[lanes, start : start + width], NT)
+            value = dot(values, turned_ref[start : start + width, lanes])
             if q:
                 value = acc_ref[:, lanes] + value
             if q == tip:
-                store_part(1, i, value)
-                core_copy(1, i).start()
-                if i > 0:
-                    exchange(1, i - 1)
+                store_part(final, i, value)
             else:
                 acc_ref[:, lanes] = value
 
     def store_part(group, i, value):
+        first, stop = spans[group]
+        size = stop - first
+        value = value[: size * batch]
         if slab % 8 == 0:
             split = value.reshape(size, nc, nx, slab, block).astype(bf16)
             for e in range(nc):
                 for h in range(nx):
-                    part_ref[group, i, e, h] = split[:, e, h]
+                    part_ref[i, e, h, first:stop] = split[:, e, h]
         else:
             for n in range(size):
                 for e in range(nc):
                     for h in range(nx):
-                        first = ((n * nc + e) * nx + h) * slab
-                        part_ref[group, i, e, h, n] = value[first : first + slab].astype(bf16)
+                        row = ((n * nc + e) * nx + h) * slab
+                        part_ref[i, e, h, first + n] = value[row : row + slab].astype(bf16)
+        core_copy(group, i).start()
+
+    def span_of(group):
+        first, stop = spans[group]
+        return pl.ds(first, stop - first)
 
     def core_copy(group, i):
+        span = span_of(group)
         return remote(
-            part_ref.at[group, i, 1 - c], sibling_ref.at[group, i], cs, cr.at[group, i], sibling
+            part_ref.at[i, 1 - c, :, span],
+            sibling_ref.at[i, :, span],
+            cs,
+            cr.at[group, i],
+            sibling,
         )
 
     def pair_copy(group, i, d):
+        span = span_of(group)
         return remote(
-            pair_ref.at[group, i, d - 1],
-            peer_ref.at[group, i, d - 1],
+            pair_ref.at[i, d - 1, span],
+            peer_ref.at[i, d - 1, span],
             xs.at[d - 1],
             xr.at[group, i, d - 1],
             x_peers[d - 1],
         )
 
     def exchange(group, i):
+        span = slice(*spans[group])
         core_copy(group, i).wait_recv()
         for d in range(1, nx):
             column = lax.rem(x + d, nx)
-            pair_ref[group, i, d - 1] = (
-                part_ref[group, i, c, column].astype(f32)
-                + sibling_ref[group, i, column].astype(f32)
+            pair_ref[i, d - 1, span] = (
+                part_ref[i, c, column, span].astype(f32)
+                + sibling_ref[i, column, span].astype(f32)
             ).astype(bf16)
             pair_copy(group, i, d).start()
 
     def collect(group, i):
+        first, stop = spans[group]
+        span = slice(first, stop)
         for d in range(1, nx):
             pair_copy(group, i, d).wait_recv()
-        value = part_ref[group, i, c, x].astype(f32) + sibling_ref[group, i, x].astype(f32)
+        value = part_ref[i, c, x, span].astype(f32) + sibling_ref[i, x, span].astype(f32)
         for d in range(1, nx):
-            value = value + peer_ref[group, i, d - 1].astype(f32)
-        total_ref[group, i] = value.astype(bf16)
-        for n in reversed(range(size)):
-            if group or n:
+            value = value + peer_ref[i, d - 1, span].astype(f32)
+        total_ref[i, span] = value.astype(bf16)
+        for n in reversed(range(first, stop)):
+            if n:
                 remote(
-                    total_ref.at[group, i, n], back_ref.at[g, i], gs, gr, (groups[group][n], t)
+                    total_ref.at[i, n], back_ref.at[g, i], gs, gr, (members[n], t)
                 ).start()
             else:
-                back_ref[g, i] = total_ref[group, i, n]
-
-    def part_product(i, late_half):
-        middle = cols // 2
-        lanes = slice(middle, cols) if late_half else slice(0, middle)
-        rows_here = slice(i * block, (i + 1) * block)
-        value = dot(
-            gathered(0, lanes.start, middle), density_ref[rows_here, lanes], NT
+                back_ref[g, i] = total_ref[i, n]
+
+    def group_product(group, i):
+        if i == 0:
+            for line in lines[group]:
+                if line:
+                    take_across(line)
+        store_part(
+            group,
+            i,
+            dot(
+                gathered(group, 0, cols), turned_ref[:, i * block : (i + 1) * block]
+            ),
         )
-        if not late_half:
-            half_ref[...] = value
-            return
-        store_part(0, i, half_ref[...] + value)
-        core_copy(0, i).start()
-        if i > 0:
-            exchange(0, i - 1)
-
-    def begin():
-        density_load.wait()
-        for i in range(1, half):
-            take_across(i)
-
-    items = [begin]
-    for i in range(row_blocks):
-        items += [functools.partial(part_product, i, e) for e in range(2)]
-    after = [functools.partial(exchange, 0, row_blocks - 1)]
-    after += [functools.partial(collect, 0, i) for i in range(row_blocks)]
-
-    def pump(work, count=1):
-        for _ in range(min(count, len(work))):
-            work.pop(0)()
-
-    done = 0
+        if i > 1:
+            exchange(group, i - 2)
+
+    items, after = [], []
+
+    def enqueue(group):
+        items.extend(functools.partial(group_product, group, i) for i in range(row_blocks))
+        for i in range(max(0, row_blocks - 2), row_blocks):
+            items.append(functools.partial(exchange, group, i))
+        after.extend(functools.partial(collect, group, i) for i in range(row_blocks))
+
     share(z, 0)
     for step in range(1, nz):
         for q in range(chunks):
             serve(step, q, (0,))
             send_across(step, order[step], q)
-            if (step, q) == (half, chunks // 2 - 1):
-                pump(items)
-            if (step, q) >= (half, chunks // 2 - 1):
-                pump(items)
-            if step == nz - 1 and q >= LAG:
-                pump(items, len(items))
-                multiply(done)
-                done += 1
-                if q > LAG:
-                    pump(after)
+            pump(turns, 3)
+            if (step, q) == (half, chunks // 2 + 1):
+                pump(turns, len(turns))
+                enqueue(0)
+            if half < step and q == 2:
+                enqueue(step - half)
+            if step == nz - 1 and q >= 4:
+                pump(after)
+            pump(items)
         serve(step, tip, range(1, ny))
         if step == 1:
             take_across(0)
         if step < nz - 1:
             share(order[step], 0)
     pump(items, len(items))
-    while done < tip:
-        multiply(done)
-        done += 1
-        pump(after)
+    for q in range(chunks):
+        multiply(q)
+    for i in range(row_blocks):
+        exchange(final, i)
     pump(after, len(after))
-    multiply(tip)
-    exchange(1, row_blocks - 1)
     for i in range(row_blocks):
-        collect(1, i)
-
-    for i in range(half, nz):
-        if i == nz - 1:
-            share(order[i], 0)
-        for d in range(1, ny):
-            share(order[i], d)
+        collect(final, i)
+
+    for d in range(ny):
+        share(order[nz - 1], d)
 
     own_rows = pltpu.make_async_copy(
         all_ref.at[:, :, pl.ds(row_start, rows)], rows_ref, local_sem
@@ -638,7 +677,7 @@
 
     drain(sibling_ref, cs)
     for d in range(1, nx):
-        drain(pair_ref.at[:, :, d - 1], xs.at[d - 1])
+        drain(pair_ref.at[:, d - 1], xs.at[d - 1])
     drain(back_ref.at[pl.ds(0, grid_count - 1)], gs)
     drain(pot_ref, vs)
     drain(send_ref, ws)
@@ -669,25 +708,28 @@
     strip = lmo_coeffs.shape[1] // tile_count
     tile_blocks, row_blocks, chunks = cols // block, rows // block, len(column_cuts(cols))
     dma = pltpu.SemaphoreType.DMA
-    smem = pl.BlockSpec(memory_space=pltpu.SMEM)
     vmem = pl.BlockSpec(memory_space=pltpu.VMEM)
     anywhere = pl.BlockSpec(memory_space=pltpu.HBM)
     side = max(1, ny - 1)
-    size = nz // 2 * ny
+    groups = 1 + nz - nz // 2
     return pl.pallas_call(
         functools.partial(kernel, nz, ny, nx),
         out_shape=jax.ShapeDtypeStruct((strip, rows), bf16),
-        in_specs=[smem, smem, vmem] + [anywhere] * 7,
+        in_specs=[anywhere] * 10,
         out_specs=vmem,
         scratch_shapes=[
+            pltpu.SMEM(sig_blocks.shape, jnp.int32),
+            pltpu.SMEM(domain_blocks.shape, jnp.int32),
+            pltpu.VMEM((batch, cols), bf16),
             pltpu.VMEM((grid_count, batch, cols), bf16),
-            pltpu.VMEM((rows, cols), bf16),
-            pltpu.VMEM((size * batch, rows), f32),
-            pltpu.VMEM((2, row_blocks, nc, nx, size, slab, block), bf16),
-            pltpu.VMEM((2, row_blocks, nx, size, slab, block), bf16),
-            pltpu.VMEM((2, row_blocks, max(1, nx - 1), size, slab, block), bf16),
-            pltpu.VMEM((2, row_blocks, max(1, nx - 1), size, slab, block), bf16),
-            pltpu.VMEM((2, row_blocks, size, slab, block), bf16),
+            pltpu.VMEM((2, block, cols), bf16),
+            pltpu.VMEM((cols, rows), bf16),
+            pltpu.VMEM((ny * batch, rows), f32),
+            pltpu.VMEM((row_blocks, nc, nx, grid_count, slab, block), bf16),
+            pltpu.VMEM((row_blocks, nx, grid_count, slab, block), bf16),
+            pltpu.VMEM((row_blocks, max(1, nx - 1), grid_count, slab, block), bf16),
+            pltpu.VMEM((row_blocks, max(1, nx - 1), grid_count, slab, block), bf16),
+            pltpu.VMEM((row_blocks, grid_count, slab, block), bf16),
             pltpu.VMEM((grid_count, row_blocks, slab, block), bf16),
             pltpu.VMEM(coulomb_core.shape, bf16),
             pltpu.VMEM(screen_mask.shape, jnp.int32),
@@ -707,24 +749,23 @@
             pltpu.VMEM((grid_count, batch, strip), bf16),
             pltpu.VMEM((grid_count, batch, rows), bf16),
             pltpu.SMEM((domain_blocks.shape[0], tile_blocks), f32),
-            pltpu.VMEM((size * batch, block), f32),
             pltpu.VMEM((nx, nc, batch, strip), f32),
             dma((2, nz)),
             dma((nz - 1, chunks)),
             dma((2, nz, side)),
             dma((nz - 1, side)),
             dma((side, nz + 1)),
-            dma((side, nz // 2)),
+            dma((side, nz - 1)),
             dma((side, chunks - 1)),
             dma((side,)),
             dma((nx,)),
             dma((grid_count,)),
             dma,
-            dma((7,)),
-            dma,
-            dma((2, row_blocks)),
+            dma((11,)),
+            dma,
+            dma((groups, row_blocks)),
             dma((max(1, nx - 1),)),
-            dma((2, row_blocks, max(1, nx - 1))),
+            dma((groups, row_blocks, max(1, nx - 1))),
             dma,
             dma,
             dma,

time: 57.4 us -> 53.5 us (0.932)
  Pallas kernels: 56.2 us -> 52.3 us
    pallas_call x1, Pallas kernels: 56.2 us -> 52.3 us  [shards(): pl.pallas_call(functools.partial(kernel, nz, ny, nx), out_shape=jax.Shape...]
where the time goes in v3:
time: 53.5 us; the launch traced here: 53.3 us
  Pallas kernels  52.3 us (98%)
  local copies, waits for them, and re-layouts  0.97 us (2%)
    pallas_call x1, Pallas kernels, shards(): pl.pallas_call(functools.partial(kernel, nz, ny, nx), out_shape=jax.Shape...  52.3 us

profile of v3, /device:TPU:0, one launch (start us, length us, event | category | flops | bytes accessed | tf_op | source)
XLA Modules:
  0.0 53.3 jit_solution(6588862187547642701)
XLA Ops:
  0.0 52.3 %shard_map.100 = bf16[256,2048]{1,0:T(8,128)(2,1)S(1)} custom-call(s32[1,16]{1,0:T(1,128)} %sig_hbm.1, s32[4,16]{1,0:T(4,128)} %domain_hbm.1, bf16[32,4096]{1,0:T(8,128)(2,1)} %value_hbm.1, bf16[2048,4096]{1,0:T(8,128)(2,1)} %density_hbm.1, bf16[512,512]{1,0:T(8,128)(2,1)} %core_hbm.1, s32[32,32]{1,0:T(8,128)} %mask_hbm.1, f32[3,16384]{1,0:T(4,128)} %centers_hbm.1, ...), custom_call_target="tpu_custom_call" | custom-call | tf_op jit(solution)/shard_map/pallas_call | solution.py:715
  52.3 1.0 %copy.12 = bf16[256,2048]{1,0:T(8,128)(2,1)} copy(bf16[256,2048]{1,0:T(8,128)(2,1)S(1)} %shard_map.100) | data formatting | bytes 2097152

commit v4 on v3

--- a/solution.py
+++ b/solution.py
@@ -331,6 +331,11 @@
         return jnp.where(i <= 2 * near, paired, single)
 
     order = [nearest(i) for i in range(nz)]
+    inner = near > 0
+    if nz > 2:
+        order[-2:] = [
+            jnp.where(inner, order[-1], order[-2]), jnp.where(inner, order[-2], order[-1])
+        ]
 
     row_start = pl.multiple_of((g * rows) % cols, rows)
     owner = (g * rows) // cols
@@ -375,31 +380,44 @@
     lines = [list(range(half))] + [[i] for i in range(half, nz)]
     spans = [(group[0] * ny, (group[-1] + 1) * ny) for group in lines]
     final = len(lines) - 1
+    early_part = tip // 2 + 1
+    sequence = [
+        part
+        for part in (
+            list(range(min(early_part, tip - 1))),
+            list(range(early_part, tip - 1)),
+            [tip],
+            [tip - 1],
+        )
+        if part
+    ]
 
     def gathered(group, start, width):
         first, stop = spans[group]
         sources = members[first:stop]
-        if group != final:
+        if group != final or width > 2 * CHUNK:
             sources = sources * max(1, FILL // ((stop - first) * batch))
         return jnp.concatenate(
             [all_ref[src, :, start : start + width] for src in sources], axis=0
         )
 
-    def multiply(q):
-        start, width = cuts[q]
-        if q != tip:
-            for d in range(1, ny):
-                arrived(piece(0, q), yl.at[d - 1, q])
+    def multiply(part):
+        start = cuts[part[0]][0]
+        width = sum(cuts[q][1] for q in part)
+        for q in part:
+            if q != tip:
+                for d in range(1, ny):
+                    arrived(piece(0, q), yl.at[d - 1, q])
         values = gathered(final, start, width)
         for i in range(row_blocks):
             lanes = slice(i * block, (i + 1) * block)
             value = dot(values, turned_ref[start : start + width, lanes])
-            if q:
-                value = acc_ref[:, lanes] + value
-            if q == tip:
+            if part is not sequence[0]:
+                value = acc_ref[:, lanes] + value[: acc_ref.shape[0]]
+            if part is sequence[-1]:
                 store_part(final, i, value)
             else:
-                acc_ref[:, lanes] = value
+                acc_ref[:, lanes] = value[: acc_ref.shape[0]]
 
     def store_part(group, i, value):
         first, stop = spans[group]
@@ -497,15 +515,26 @@
     for step in range(1, nz):
         for q in range(chunks):
             serve(step, q, (0,))
-            send_across(step, order[step], q)
+            if step < nz - 1:
+                send_across(step, order[step], q)
+            else:
+                if q == 0:
+
+                    @pl.when(inner)
+                    def _():
+                        for ahead in range(tip):
+                            send_across(step, order[step], ahead)
+
+                @pl.when(jnp.logical_not(inner))
+                def _():
+                    send_across(step, order[step], q)
+
             pump(turns, 3)
             if (step, q) == (half, chunks // 2 + 1):
                 pump(turns, len(turns))
                 enqueue(0)
             if half < step and q == 2:
                 enqueue(step - half)
-            if step == nz - 1 and q >= 4:
-                pump(after)
             pump(items)
         serve(step, tip, range(1, ny))
         if step == 1:
@@ -513,8 +542,10 @@
         if step < nz - 1:
             share(order[step], 0)
     pump(items, len(items))
-    for q in range(chunks):
-        multiply(q)
+    for part in sequence:
+        multiply(part)
+        if part is not sequence[-1]:
+            pump(after, 2)
     for i in range(row_blocks):
         exchange(final, i)
     pump(after, len(after))
@@ -592,7 +623,10 @@
             axis=0,
         )
         start = pl.multiple_of(plane * group_width, group_width)
-        values = dot(kept, lmo_ref[:, pl.ds(start, group_width)])
+        copies = max(1, FILL // kept.shape[0])
+        values = dot(
+            jnp.concatenate([kept] * copies, axis=0), lmo_ref[:, pl.ds(start, group_width)]
+        )
         pieces = []
         for e in range(nc):
             parts = []

time: 53.5 us -> 51.7 us (0.966)
  Pallas kernels: 52.3 us -> 50.5 us
    pallas_call x1, Pallas kernels: 52.3 us -> 50.5 us  [shards(): pl.pallas_call(functools.partial(kernel, nz, ny, nx), out_shape=jax.Shape...]
where the time goes in v4:
time: 51.7 us; the launch traced here: 51.5 us
  Pallas kernels  50.5 us (98%)
  local copies, waits for them, and re-layouts  0.97 us (2%)
    pallas_call x1, Pallas kernels, shards(): pl.pallas_call(functools.partial(kernel, nz, ny, nx), out_shape=jax.Shape...  50.5 us

profile of v4, /device:TPU:0, one launch (start us, length us, event | category | flops | bytes accessed | tf_op | source)
XLA Modules:
  0.0 51.5 jit_solution(2619728408849134373)
XLA Ops:
  0.0 50.5 %shard_map.100 = bf16[256,2048]{1,0:T(8,128)(2,1)S(1)} custom-call(s32[1,16]{1,0:T(1,128)} %sig_hbm.1, s32[4,16]{1,0:T(4,128)} %domain_hbm.1, bf16[32,4096]{1,0:T(8,128)(2,1)} %value_hbm.1, bf16[2048,4096]{1,0:T(8,128)(2,1)} %density_hbm.1, bf16[512,512]{1,0:T(8,128)(2,1)} %core_hbm.1, s32[32,32]{1,0:T(8,128)} %mask_hbm.1, f32[3,16384]{1,0:T(4,128)} %centers_hbm.1, ...), custom_call_target="tpu_custom_call" | custom-call | tf_op jit(solution)/shard_map/pallas_call | solution.py:749
  50.6 1.0 %copy.12 = bf16[256,2048]{1,0:T(8,128)(2,1)} copy(bf16[256,2048]{1,0:T(8,128)(2,1)S(1)} %shard_map.100) | data formatting | bytes 2097152

commit v5 on v4

--- a/solution.py
+++ b/solution.py
@@ -82,6 +82,7 @@
     total_ref,
     back_ref,
     core_ref,
+    mix_ref,
     mask_ref,
     centers_ref,
     widths_ref,
@@ -276,7 +277,12 @@
             if i == row_blocks - 1:
                 lmo_load.start()
 
+    def turn_core():
+        core_load.wait()
+        mix_ref[...] = core_ref[...].T
+
     turns = [functools.partial(turn, i, k) for i in range(row_blocks) for k in range(tile_blocks)]
+    turns.append(turn_core)
 
     def pump(work, count=1):
         for _ in range(min(count, len(work))):
@@ -563,7 +569,6 @@
     def _():
         own_rows.start()
 
-    core_load.wait()
     def wait_all(spot, recv):
         remote(spot, spot, gs, recv, right).wait_recv()
 
@@ -579,7 +584,7 @@
     for n, tile in enumerate(tile_order):
         span = pl.ds(pl.multiple_of(tile * tile_rows, tile_rows), tile_rows)
         screened = dot(spread_ref[span, :], weighted).astype(bf16)
-        potential = scaled_ref[span, :] * dot(screened, core_ref[...], NT)
+        potential = scaled_ref[span, :] * dot(screened, mix_ref[...])
         is_own = n == len(tile_order) - 1
         for m in range(tile_blocks):
             value = potential[m * slab : (m + 1) * slab, :].astype(bf16)
@@ -766,6 +771,7 @@
             pltpu.VMEM((row_blocks, grid_count, slab, block), bf16),
             pltpu.VMEM((grid_count, row_blocks, slab, block), bf16),
             pltpu.VMEM(coulomb_core.shape, bf16),
+            pltpu.VMEM(coulomb_core.shape, bf16),
             pltpu.VMEM(screen_mask.shape, jnp.int32),
             pltpu.VMEM(ao_centers.shape, f32),
             pltpu.VMEM((1, total), f32),

time: 51.7 us -> 51.6 us (level)
  no operation moved by 1% of the time
where the time goes in v5:
time: 51.6 us; the launch traced here: 51.5 us
  Pallas kernels  50.5 us (98%)
  local copies, waits for them, and re-layouts  0.97 us (2%)
    pallas_call x1, Pallas kernels, shards(): pl.pallas_call(functools.partial(kernel, nz, ny, nx), out_shape=jax.Shape...  50.5 us

profile of v5, /device:TPU:0, one launch (start us, length us, event | category | flops | bytes accessed | tf_op | source)
XLA Modules:
  0.0 51.5 jit_solution(16885597845882001208)
XLA Ops:
  0.0 50.5 %shard_map.100 = bf16[256,2048]{1,0:T(8,128)(2,1)S(1)} custom-call(s32[1,16]{1,0:T(1,128)} %sig_hbm.1, s32[4,16]{1,0:T(4,128)} %domain_hbm.1, bf16[32,4096]{1,0:T(8,128)(2,1)} %value_hbm.1, bf16[2048,4096]{1,0:T(8,128)(2,1)} %density_hbm.1, bf16[512,512]{1,0:T(8,128)(2,1)} %core_hbm.1, s32[32,32]{1,0:T(8,128)} %mask_hbm.1, f32[3,16384]{1,0:T(4,128)} %centers_hbm.1, ...), custom_call_target="tpu_custom_call" | custom-call | tf_op jit(solution)/shard_map/pallas_call | solution.py:754
  50.5 1.0 %copy.12 = bf16[256,2048]{1,0:T(8,128)(2,1)} copy(bf16[256,2048]{1,0:T(8,128)(2,1)S(1)} %shard_map.100) | data formatting | bytes 2097152
